TPU v7x, 256 devices: a whole 4x4x8 slice. The times are simulated.
256 devices in a mesh: ty: 8 (over y, z_hi), tx: 16 (over x, z_lo), pa: 2 (over core).
Axes of the slice: x: 4, y: 4, z: 8 (z_hi: 2, z_lo: 4; z = z_hi * 4 + z_lo), core: 2. Of those that a mesh axis runs over, the one named last changes fastest.
Arguments:
- object_field: float32 [2, 8192, 4096], P(None, 'ty', 'tx'), may hold values from -6 to 6
- probe_field: float32 [2, 128, 128], replicated, may hold values from -6 to 6
- amplitudes: bfloat16 [8, 16, 128, 128, 128], P('ty', 'tx', 'pa'), may hold values from 0.049804688 to 1.5
- start_row: int32 [8, 16, 128], P('ty', 'tx', 'pa'), may hold values from 0 to 1023
- start_col: int32 [8, 16, 128], P('ty', 'tx', 'pa'), may hold values from 0 to 255
- counts: int32 [8, 16], replicated, may hold values from 16 to 96, as said below
Outputs:
- object_grad: float32 [2, 8192, 4096], P(None, 'ty', 'tx')
- probe_grad: float32 [2, 128, 128], replicated
Inputs may be any that keep to these rules, and one draw needn't show every extreme that they name: Tile (a, b) uses its first counts[a, b] slots; some tile uses exactly 96.
All inputs are finite; a program needn't handle non-finite values.
Results may differ from a plain program's by a relative error of at most 0.0007.
The roundings to bfloat16 on the way count: a program that leaves them out, or rounds other values in their place, can miss the bound.
Values may be sent and summed in bfloat16 or wider, within the bound.
A program may use at most 64 MiB of HBM per device.

v0:
```python
import math

import jax
import jax.numpy as jnp
from jax import lax
from jax.sharding import PartitionSpec as P

BLK = 8


def from_behind(value, axis, steps):
    count = lax.axis_size(axis)
    initial, last = (max(0, -steps), min(count, count - steps))
    return lax.ppermute(value, axis, [(source, source + steps) for source in range(initial, last)])


def dft_table(length, inverse):
    freqs = jnp.arange(length, dtype=jnp.int32)
    phase = freqs[:, None] * freqs[None, :] % length
    angle = phase.astype(jnp.float32) * (2.0 * math.pi / length)
    scale = 1.0 / math.sqrt(length)
    cosine = jnp.cos(angle) * scale
    sine = jnp.sin(angle) * scale
    if inverse:
        upper = jnp.concatenate([cosine, sine], axis=1)
        lower = jnp.concatenate([-sine, cosine], axis=1)
    else:
        upper = jnp.concatenate([cosine, -sine], axis=1)
        lower = jnp.concatenate([sine, cosine], axis=1)
    return jnp.concatenate([upper, lower], axis=0).astype(jnp.bfloat16)


def along_last(real_part, imag_part, table):
    length = real_part.shape[-1]
    stacked = jnp.concatenate([real_part, imag_part], axis=-1)
    result = jnp.einsum("bnk,kj->bnj", stacked, table, preferred_element_type=jnp.float32)
    return (result[..., :length], result[..., length:])


def patch_terms(patches, measured, probe_field, usable, forward_table, inverse_table):
    probe_re = probe_field[0]
    probe_im = probe_field[1]
    patch_re = patches[:, 0]
    patch_im = patches[:, 1]
    psi_re = (probe_re * patch_re - probe_im * patch_im).astype(jnp.bfloat16)
    psi_im = (probe_re * patch_im + probe_im * patch_re).astype(jnp.bfloat16)
    half_re, half_im = along_last(psi_re, psi_im, forward_table)
    half_re = jnp.swapaxes(half_re.astype(jnp.bfloat16), 1, 2)
    half_im = jnp.swapaxes(half_im.astype(jnp.bfloat16), 1, 2)
    wave_re, wave_im = along_last(half_re, half_im, forward_table)
    level = jnp.swapaxes(measured, 1, 2).astype(jnp.float32)
    modulus = jnp.sqrt(wave_re * wave_re + wave_im * wave_im + 1.0)
    factor = jnp.where(usable[:, None, None], 1.0 - level / modulus, 0.0)
    chi_re = (wave_re * factor).astype(jnp.bfloat16)
    chi_im = (wave_im * factor).astype(jnp.bfloat16)
    back_re, back_im = along_last(chi_re, chi_im, inverse_table)
    back_re = jnp.swapaxes(back_re.astype(jnp.bfloat16), 1, 2)
    back_im = jnp.swapaxes(back_im.astype(jnp.bfloat16), 1, 2)
    grad_re, grad_im = along_last(back_re, back_im, inverse_table)
    object_re = probe_re * grad_re + probe_im * grad_im
    object_im = probe_re * grad_im - probe_im * grad_re
    probe_part_re = jnp.sum(patch_re * grad_re + patch_im * grad_im, axis=0)
    probe_part_im = jnp.sum(patch_re * grad_im - patch_im * grad_re, axis=0)
    return (object_re, object_im, jnp.stack([probe_part_re, probe_part_im]))


def shards(object_field, probe_field, amplitudes, start_row, start_col, counts):
    width = probe_field.shape[-1]
    tile_height = object_field.shape[1]
    tile_width = object_field.shape[2]
    half = start_row.shape[-1]
    row_place = lax.axis_index("ty")
    col_place = lax.axis_index("tx")
    core_place = lax.axis_index("pa")
    count = counts[row_place, col_place]
    zero = jnp.int32(0)
    right = from_behind(object_field[:, :, :width], "tx", -1)
    wider = jnp.concatenate([object_field, right], axis=2)
    below = from_behind(wider[:, :width, :], "ty", -1)
    extended = jnp.concatenate([wider, below], axis=1)
    rows_list = start_row[0, 0]
    cols_list = start_col[0, 0]
    measured_list = amplitudes[0, 0]
    nvalid = jnp.clip(count - core_place * half, 0, half)
    forward_table = dft_table(width, False)
    inverse_table = dft_table(width, True)

    def block_step(block_index, carry):
        grad_field, probe_acc = carry
        first = block_index * BLK
        block_rows = lax.dynamic_slice_in_dim(rows_list, first, BLK)
        block_cols = lax.dynamic_slice_in_dim(cols_list, first, BLK)
        measured = lax.dynamic_slice_in_dim(measured_list, first, BLK)
        usable = first + jnp.arange(BLK, dtype=jnp.int32) < nvalid
        patches = jnp.stack(
            [
                lax.dynamic_slice(
                    extended, (zero, block_rows[member], block_cols[member]), (2, width, width)
                )
                for member in range(BLK)
            ]
        )
        object_re, object_im, probe_part = patch_terms(
            patches, measured, probe_field, usable, forward_table, inverse_table
        )
        for member in range(BLK):
            where_at = (zero, block_rows[member], block_cols[member])
            current = lax.dynamic_slice(grad_field, where_at, (2, width, width))
            added = current + jnp.stack([object_re[member], object_im[member]])
            grad_field = lax.dynamic_update_slice(grad_field, added, where_at)
        return (grad_field, probe_acc + probe_part)

    nblocks = (nvalid + BLK - 1) // BLK
    init = (jnp.zeros(extended.shape, jnp.float32), jnp.zeros((2, width, width), jnp.float32))
    grad_field, probe_acc = lax.fori_loop(0, nblocks, block_step, init)
    right_strip = grad_field[:, :, tile_width:]
    arrived = from_behind(right_strip, "tx", 1)
    grad_field = grad_field[:, :, :tile_width].at[:, :, :width].add(arrived)
    lower_strip = grad_field[:, tile_height:, :]
    arrived_below = from_behind(lower_strip, "ty", 1)
    tile_grad = grad_field[:, :tile_height, :].at[:, :width, :].add(arrived_below)
    object_grad = lax.psum(tile_grad, "pa")
    probe_total = lax.psum(probe_acc, ("ty", "tx", "pa"))
    probe_grad = probe_total / jnp.sum(counts).astype(jnp.float32)
    return (object_grad, probe_grad)


def solution(mesh):
    return jax.shard_map(
        shards,
        mesh=mesh,
        in_specs=(
            P(None, "ty", "tx"),
            P(),
            P("ty", "tx", "pa", None, None),
            P("ty", "tx", "pa"),
            P("ty", "tx", "pa"),
            P(),
        ),
        out_specs=(P(None, "ty", "tx"), P()),
        check_vma=False,
    )
```

profile of v0, /device:TPU:1, one launch (start us, length us, event | category | flops | bytes accessed | tf_op | source)
XLA Modules:
  0.0 1033.9 jit_solution(16384427669747535714)
XLA Ops:
  7.2 0.0 all-reduce.5.cloned.1.call-start
  7.2 1.4 slice.220
  8.7 1.3 collective-permute-start
  10.0 0.1 constant_dynamic-update-slice_fusion.1
  10.1 23.9 %collective-permute-done = f32[2,1024,128]{2,1,0:T(8,128)S(1)} collective-permute-done((f32[2,1024,128]{2,1,0:T(8,128)S(1)}, f32[2,1024,128]{2,1,0:T(8,128)S(1)}, u32[]{:S(2)}, u32[]{:S(2)}) %collective-permute-start) | collective-permute-done | bytes 1048608 | tf_op jit(solution)/shard_map/ppermute | solution.py:14
  34.0 0.1 constant_dynamic-update-slice_fusion
  34.1 1.7 copy-done
  35.8 1.3 collective-permute-start.1
  37.1 0.6 dynamic_slice.60
  38.4 3.2 copy.10
  41.6 0.3 fusion.33
  41.9 0.3 negate_convert_fusion
  42.2 11.7 %collective-permute-done.1 = f32[2,128,384]{2,1,0:T(8,128)S(1)} collective-permute-done((f32[2,128,384]{2,1,0:T(8,128)S(1)}, f32[2,128,384]{2,1,0:T(8,128)S(1)}, u32[]{:S(2)}, u32[]{:S(2)}) %collective-permute-start.1) | collective-permute-done | bytes 393248 | tf_op jit(solution)/shard_map/ppermute | solution.py:14
  53.9 3.9 pad_maximum_fusion
  57.8 2.0 broadcast_in_dim.23
  59.9 1.4 slice.224
  61.3 11.1 %collective-permute-start.2 = (f32[2,1152,128]{2,1,0:T(8,128)S(1)}, f32[2,1152,128]{2,1,0:T(8,128)S(1)}, u32[]{:S(2)}, u32[]{:S(2)}) collective-permute-start(f32[2,1152,128]{2,1,0:T(8,128)S(1)} %slice.224), channel_id=1, source_target_pairs={{0,2},{2,4},{4,6},{6,8},{8,10},{10,12},{12,14},{14,16},{16,18},{18... | collective-permute-start | bytes 3538952 | tf_op jit(solution)/shard_map/ppermute | solution.py:14
  72.4 1.8 slice.222
  74.3 11.2 %collective-permute-done.2 = f32[2,1152,128]{2,1,0:T(8,128)S(1)} collective-permute-done((f32[2,1152,128]{2,1,0:T(8,128)S(1)}, f32[2,1152,128]{2,1,0:T(8,128)S(1)}, u32[]{:S(2)}, u32[]{:S(2)}) %collective-permute-start.2) | collective-permute-done | bytes 1179680 | tf_op jit(solution)/shard_map/ppermute | solution.py:14
  85.5 1.4 add_dynamic-update-slice_fusion
  86.9 327.0 %collective-permute-start.3 = (f32[2,128,256]{2,1,0:T(8,128)S(1)}, f32[2,128,256]{2,1,0:T(8,128)S(1)}, u32[]{:S(2)}, u32[]{:S(2)}) collective-permute-start(f32[2,128,256]{2,1,0:T(8,128)S(1)} %slice.257), channel_id=1, source_target_pairs={{0,32},{32,64},{64,96},{96,128},{128,160},{160,192},{192,224},{1,3... | collective-permute-start | bytes 786440 | tf_op jit(solution)/shard_map/ppermute | solution.py:14
  413.9 0.0 all-reduce.5.cloned.1.call-update
  413.9 0.0 all-reduce.3.cloned.1.call-start
  414.0 1.5 slice.255
  415.4 1.8 collective-permute-done.3
  417.2 0.7 fusion.24
  417.9 0.0 all-reduce.3.cloned.1.call-update
  417.9 0.7 reduce_sum.27
  419.2 571.3 %all-reduce.5.cloned.1.call-done = f32[2,128,128]{2,1,0:T(8,128)} async-done(((f32[2,128,128]{2,1,0:T(8,128)}), f32[2,128,128]{2,1,0:T(8,128)}) %all-reduce.5.cloned.1.call-update) | async-done | bytes 131088 | tf_op jit(solution)/shard_map/psum | solution.py:123
  990.5 1.6 broadcast_divide_fusion
  992.1 32.0 %all-reduce.3.cloned.1.call-done = f32[2,1024,256]{2,1,0:T(8,128)} async-done(((f32[2,1024,256]{2,1,0:T(8,128)}), f32[2,1024,256]{2,1,0:T(8,128)}) %all-reduce.3.cloned.1.call-update) | async-done | bytes 2097168 | tf_op jit(solution)/shard_map/psum | solution.py:122
  1024.0 3.0 copy.42
  (16 shorter events, 0.1 us)
Async XLA Ops:
  7.2 2.8 copy-start.2
  7.2 983.3 %all-reduce.5.cloned.1.call-start = ((), (), s32[]{:S(2)}) async-start(), calls=%async_computation.1 | async-start | bytes 262144 | tf_op jit(solution)/shard_map/psum | solution.py:123
  8.7 28.4 %copy-start.5 = (s32[8,16]{1,0:T(8,128)S(1)}, s32[8,16]{1,0:T(8,128)}, u32[]{:S(2)}) copy-start(s32[8,16]{1,0:T(8,128)} %param.17) | copy-start | bytes 1540
  8.7 25.3 %collective-permute-start = (f32[2,1024,128]{2,1,0:T(8,128)S(1)}, f32[2,1024,128]{2,1,0:T(8,128)S(1)}, u32[]{:S(2)}, u32[]{:S(2)}) collective-permute-start(f32[2,1024,128]{2,1,0:T(8,128)S(1)} %slice.220), channel_id=1, source_target_pairs={{2,0},{4,2},{6,4},{8,6},{10,8},{12,10},{14,12},{16,14},{18,16},{20... | collective-permute-start | bytes 3145736 | tf_op jit(solution)/shard_map/ppermute | solution.py:14
  34.1 1.7 copy-start
  35.8 18.1 %collective-permute-start.1 = (f32[2,128,384]{2,1,0:T(8,128)S(1)}, f32[2,128,384]{2,1,0:T(8,128)S(1)}, u32[]{:S(2)}, u32[]{:S(2)}) collective-permute-start(f32[2,128,384]{2,1,0:T(8,128)S(1)} %slice.254), channel_id=1, source_target_pairs={{32,0},{64,32},{96,64},{128,96},{160,128},{192,160},{224,192},{33,... | collective-permute-start | bytes 1179656 | tf_op jit(solution)/shard_map/ppermute | solution.py:14
  57.8 2.1 copy-start.6
  57.8 2.1 copy-start.7
  59.9 14.4 %copy-start.1 = (f32[2,128,128]{2,1,0:T(8,128)}, f32[2,128,128]{2,1,0:T(8,128)S(1)}, u32[]{:S(2)}) copy-start(f32[2,128,128]{2,1,0:T(8,128)S(1)} %get-tuple-element.91) | copy-start | bytes 393220
  61.3 24.2 %collective-permute-start.2 = (f32[2,1152,128]{2,1,0:T(8,128)S(1)}, f32[2,1152,128]{2,1,0:T(8,128)S(1)}, u32[]{:S(2)}, u32[]{:S(2)}) collective-permute-start(f32[2,1152,128]{2,1,0:T(8,128)S(1)} %slice.224), channel_id=1, source_target_pairs={{0,2},{2,4},{4,6},{6,8},{8,10},{10,12},{12,14},{14,16},{16,18},{18... | collective-permute-start | bytes 3538952 | tf_op jit(solution)/shard_map/ppermute | solution.py:14
  86.9 330.3 %collective-permute-start.3 = (f32[2,128,256]{2,1,0:T(8,128)S(1)}, f32[2,128,256]{2,1,0:T(8,128)S(1)}, u32[]{:S(2)}, u32[]{:S(2)}) collective-permute-start(f32[2,128,256]{2,1,0:T(8,128)S(1)} %slice.257), channel_id=1, source_target_pairs={{0,32},{32,64},{64,96},{96,128},{128,160},{160,192},{192,224},{1,3... | collective-permute-start | bytes 786440 | tf_op jit(solution)/shard_map/ppermute | solution.py:14
  413.9 610.1 %all-reduce.3.cloned.1.call-start = ((), (), s32[]{:S(2)}) async-start(), calls=%async_computation | async-start | bytes 4194304 | tf_op jit(solution)/shard_map/psum | solution.py:122
Sparse Core Ops, SparseCore 0:
  414.0 576.4 all-reduce.4
  993.6 30.3 all-reduce.2
where the time goes:
time: 1050 us; the launch traced here: 1030 us
  waiting for transfers between devices  652 us (62%)
  starting transfers between devices  341 us (32%)
  local copies, waits for them, and re-layouts  17 us (2%)
  between operations  15.6 us (1%)
    psum x1, waiting for transfers between devices, shards(): probe_total = lax.psum(probe_acc, ('ty', 'tx', 'pa'))  571 us
    ppermute x4, starting transfers between devices, from_behind(): lax.ppermute(value, axis, [(source, source + steps) for source in range(i...  341 us
    ppermute x4, waiting for transfers between devices, from_behind(): lax.ppermute(value, axis, [(source, source + steps) for source in range(i...  48.5 us
    psum x1, waiting for transfers between devices, shards(): object_grad = lax.psum(tile_grad, 'pa')  32 us
  transfers between devices with their start and end apart: 6, of which 6 were waited for; matrix products, arithmetic and copies ran while one was open for 1% of the time, Pallas kernels for 0%

commit v1 on v0

v1 whole, which is shorter than its diff:
```python
import functools
import math

import jax
import jax.numpy as jnp
import ml_dtypes
import numpy as np
from jax import lax
from jax.experimental import pallas as pl
from jax.experimental.pallas import tpu as pltpu
from jax.sharding import PartitionSpec as P

BLK = 8

N = 128

def dft_tables(length):
    freqs = np.arange(length)
    angle = (freqs[:, None] * freqs[None, :] % length) * (2.0 * math.pi / length)
    cosine = np.cos(angle) / math.sqrt(length)
    sine = np.sin(angle) / math.sqrt(length)
    forward = np.block([[cosine, -sine], [sine, cosine]]).astype(ml_dtypes.bfloat16)
    inverse = np.block([[cosine, sine], [-sine, cosine]]).astype(ml_dtypes.bfloat16)
    return forward, inverse

def mm(a, b):
    return jnp.dot(a, b, preferred_element_type=jnp.float32)

def patch_kernel(B, rows_ref, cols_ref, lim_ref, ext_ref, probe_ref, amp_ref, fwd_ref, inv_ref,
                 acc_ref, pg_ref, patch_ref):
    acc_ref[...] = jnp.zeros_like(acc_ref)
    pg_ref[...] = jnp.zeros_like(pg_ref)
    lane = lax.broadcasted_iota(jnp.int32, (N, N), 1)
    last = lim_ref[0]

    def body(it, _):
        pos = []
        psis = []
        for b in range(B):
            i = it * B + b
            slot = jnp.minimum(i, last - 1)
            r = rows_ref[slot]
            c = cols_ref[slot]
            j = c // N
            s = c % N
            pos.append((slot, i < last, r, j, s))
            back = (N - s) % N
            high = lane >= s
            parts = []
            for p in range(2):
                v = jnp.where(high, ext_ref[p, j, pl.ds(r, N), :], ext_ref[p, j + 1, pl.ds(r, N), :])
                v = pltpu.roll(v, back, 1)
                patch_ref[b, p] = v
                parts.append(v)
            pre, pim = probe_ref[0], probe_ref[1]
            psi_re = pre * parts[0] - pim * parts[1]
            psi_im = pre * parts[1] + pim * parts[0]
            psis.append(jnp.concatenate([psi_re.astype(jnp.bfloat16), psi_im.astype(jnp.bfloat16)], axis=1))
        half = mm(jnp.concatenate(psis, axis=0), fwd_ref[...]).astype(jnp.bfloat16)
        rhs = jnp.concatenate(
            [jnp.concatenate([half[b * N:(b + 1) * N, q * N:(q + 1) * N] for b in range(B)], axis=1) for q in range(2)], axis=0)
        wave = mm(inv_ref[...], rhs)
        chis = [[], []]
        for b in range(B):
            slot, ok, r, j, s = pos[b]
            wre = wave[:N, b * N:(b + 1) * N]
            wim = wave[N:, b * N:(b + 1) * N]
            level = amp_ref[slot].astype(jnp.float32)
            use = ok.astype(jnp.float32)
            factor = (1.0 - level * lax.rsqrt(wre * wre + wim * wim + 1.0)) * use
            chis[0].append((wre * factor).astype(jnp.bfloat16))
            chis[1].append((wim * factor).astype(jnp.bfloat16))
        rhs2 = jnp.concatenate([jnp.concatenate(chis[q], axis=1) for q in range(2)], axis=0)
        bk = mm(fwd_ref[...], rhs2).astype(jnp.bfloat16)
        lhs = jnp.concatenate([jnp.concatenate([bk[q * N:(q + 1) * N, b * N:(b + 1) * N] for q in range(2)], axis=1) for b in range(B)], axis=0)
        grad = mm(lhs, inv_ref[...])
        tre = pg_ref[0]
        tim = pg_ref[1]
        for b in range(B):
            slot, ok, r, j, s = pos[b]
            gre = grad[b * N:(b + 1) * N, :N]
            gim = grad[b * N:(b + 1) * N, N:]
            pre, pim = probe_ref[0], probe_ref[1]
            qre, qim = patch_ref[b, 0], patch_ref[b, 1]
            tre = tre + (qre * gre + qim * gim)
            tim = tim + (qre * gim - qim * gre)
            obj = (pre * gre + pim * gim, pre * gim - pim * gre)
            high = lane >= s
            for p in range(2):
                o = pltpu.roll(obj[p], s, 1)
                acc_ref[p, j, pl.ds(r, N), :] += jnp.where(high, o, 0.0)
                acc_ref[p, j + 1, pl.ds(r, N), :] += jnp.where(high, 0.0, o)
        pg_ref[0] = tre
        pg_ref[1] = tim
        return 0

    lax.fori_loop(0, (last + B - 1) // B, body, 0)

def patches(rows, cols, lim, ext, probe, amp, fwd, inv, B=2):
    return pl.pallas_call(
        functools.partial(patch_kernel, B),
        out_shape=(jax.ShapeDtypeStruct(ext.shape, jnp.float32), jax.ShapeDtypeStruct((2, N, N), jnp.float32)),
        in_specs=[pl.BlockSpec(memory_space=pltpu.SMEM)] * 3 + [pl.BlockSpec(memory_space=pltpu.VMEM)] * 5,
        out_specs=(pl.BlockSpec(memory_space=pltpu.VMEM),) * 2,
        scratch_shapes=[pltpu.VMEM((B, 2, N, N), jnp.float32)],
        compiler_params=pltpu.CompilerParams(vmem_limit_bytes=48 << 20),
        name="patches",
    )(rows, cols, lim, ext, probe, amp, fwd, inv)


def from_behind(value, axis, steps):
    count = lax.axis_size(axis)
    initial, last = (max(0, -steps), min(count, count - steps))
    return lax.ppermute(value, axis, [(source, source + steps) for source in range(initial, last)])


def shards(object_field, probe_field, amplitudes, start_row, start_col, counts):
    height, width = object_field.shape[1:]
    half = start_row.shape[-1]
    row_place = lax.axis_index("ty")
    col_place = lax.axis_index("tx")
    core_place = lax.axis_index("pa")
    right = from_behind(object_field[:, :, :N], "tx", -1)
    top = jnp.concatenate([object_field[:, :N], right[:, :N]], axis=2)
    below = from_behind(top, "ty", -1)
    blocks = [object_field[:, :, q * N:(q + 1) * N] for q in range(width // N)] + [right]
    extended = jnp.stack(
        [jnp.concatenate([block, below[:, :, q * N:(q + 1) * N]], axis=1) for q, block in enumerate(blocks)], axis=1
    )
    nvalid = jnp.clip(counts[row_place, col_place] - core_place * half, 0, half)
    forward, inverse = dft_tables(N)
    grad, probe_part = patches(
        start_row[0, 0], start_col[0, 0], nvalid[None], extended, probe_field, amplitudes[0, 0],
        jnp.asarray(forward), jnp.asarray(inverse), BLK)
    arrived = from_behind(grad[:, -1], "tx", 1)
    grad = grad[:, :-1].at[:, 0].add(arrived)
    arrived_below = from_behind(grad[:, :, height:], "ty", 1)
    tile = grad[:, :, :height].at[:, :, :N].add(arrived_below)
    tile = lax.psum(tile, "pa")
    object_grad = jnp.concatenate([tile[:, q] for q in range(width // N)], axis=2)
    probe_total = lax.psum(probe_part, ("ty", "tx", "pa"))
    return object_grad, probe_total / jnp.sum(counts).astype(jnp.float32)


def solution(mesh):
    return jax.shard_map(
        shards,
        mesh=mesh,
        in_specs=(
            P(None, "ty", "tx"),
            P(),
            P("ty", "tx", "pa", None, None),
            P("ty", "tx", "pa"),
            P("ty", "tx", "pa"),
            P(),
        ),
        out_specs=(P(None, "ty", "tx"), P()),
        check_vma=False,
    )
```

time: 1050 us -> 405 us (0.39); the launches traced: 1030 us -> 404 us
  starting transfers between devices: 341 us -> 15.1 us
  waiting for transfers between devices: 652 us -> 356 us
    ppermute x4, starting transfers between devices: 341 us -> 15 us  [from_behind(): lax.ppermute(value, axis, [(source, source + steps) for source in range(i...]
    psum x2, waiting for transfers between devices: 603 us -> 299 us  [the longest x1 267 us: shards(): probe_total = lax.psum(probe_part, ('ty', 'tx', 'pa'))]
where the time goes in v1:
time: 405 us; the launch traced here: 404 us
  waiting for transfers between devices  356 us (88%)
  between operations  15.5 us (4%)
  starting transfers between devices  15.1 us (4%)
  other arithmetic  7.65 us (2%)
  local copies, waits for them, and re-layouts  7.06 us (2%)
    psum x1, waiting for transfers between devices, shards(): probe_total = lax.psum(probe_part, ('ty', 'tx', 'pa'))  267 us
    ppermute x4, waiting for transfers between devices, from_behind(): lax.ppermute(value, axis, [(source, source + steps) for source in range(i...  57.3 us
    psum x1, waiting for transfers between devices, shards(): tile = lax.psum(tile, 'pa')  32 us
    ppermute x4, starting transfers between devices, from_behind(): lax.ppermute(value, axis, [(source, source + steps) for source in range(i...  15 us
  transfers between devices with their start and end apart: 6, of which 6 were waited for; matrix products, arithmetic and copies ran while one was open for 1% of the time, Pallas kernels for 0%

profile of v1, /device:TPU:1, one launch (start us, length us, event | category | flops | bytes accessed | tf_op | source)
XLA Modules:
  0.0 404.2 jit_solution(18020276501267477899)
XLA Ops:
  7.2 0.0 all-reduce.5.cloned.1.call-start
  7.2 1.7 fusion.3
  9.0 1.3 collective-permute-start
  10.3 24.0 %collective-permute-done = f32[2,1024,128]{2,1,0:T(8,128)S(1)} collective-permute-done((f32[2,1024,128]{2,1,0:T(8,128)S(1)}, f32[2,1024,128]{2,1,0:T(8,128)S(1)}, u32[]{:S(2)}, u32[]{:S(2)}) %collective-permute-start) | collective-permute-done | bytes 1048608 | tf_op jit(solution)/shard_map/ppermute | solution.py:114
  34.3 0.8 pad_maximum_fusion.2
  35.1 1.3 collective-permute-start.1
  36.4 0.6 dynamic_slice.3
  37.6 15.9 %collective-permute-done.1 = f32[2,128,384]{2,1,0:T(8,128)} collective-permute-done((f32[2,128,384]{2,1,0:T(8,128)}, f32[2,128,384]{2,1,0:T(8,128)}, u32[]{:S(2)}, u32[]{:S(2)}) %collective-permute-start.1) | collective-permute-done | bytes 393248 | tf_op jit(solution)/shard_map/ppermute | solution.py:114
  53.5 1.1 fusion.4
  54.6 0.2 maximum_bitcast_fusion
  54.7 0.1 maximum_bitcast_fusion.2
  54.9 2.1 pad_maximum_fusion.ext_ref
  57.0 0.1 copy-done.2
  57.1 0.1 copy-done.3
  57.2 2.9 patches.1
  60.2 0.1 slice_bitcast_fusion
  60.2 11.1 %collective-permute-start.2 = (f32[2,1152,128]{2,1,0:T(8,128)S(1)}, f32[2,1152,128]{2,1,0:T(8,128)S(1)}, u32[]{:S(2)}, u32[]{:S(2)}) collective-permute-start(f32[2,1152,128]{2,1,0:T(8,128)S(1)} %slice_bitcast_fusion), channel_id=1, source_target_pairs={{0,2},{2,4},{4,6},{6,8},{8,10},{10,12},{12,14},{14,16},{16,18},{18... | collective-permute-start | bytes 3538952 | tf_op jit(solution)/shard_map/ppermute | solution.py:114
  71.4 0.2 slice.105
  71.5 12.9 %collective-permute-done.2 = f32[2,1152,128]{2,1,0:T(8,128)S(1)} collective-permute-done((f32[2,1152,128]{2,1,0:T(8,128)S(1)}, f32[2,1152,128]{2,1,0:T(8,128)S(1)}, u32[]{:S(2)}, u32[]{:S(2)}) %collective-permute-start.2) | collective-permute-done | bytes 1179680 | tf_op jit(solution)/shard_map/ppermute | solution.py:114
  84.4 0.1 fusion.1
  84.6 1.3 collective-permute-start.3
  85.9 0.0 all-reduce.5.cloned.1.call-update
  85.9 0.0 all-reduce.3.cloned.1.call-start
  86.0 1.5 slice.118
  87.4 4.6 %collective-permute-done.3 = f32[2,2,128,128]{3,2,1,0:T(8,128)S(1)} collective-permute-done((f32[2,2,128,128]{3,2,1,0:T(8,128)S(1)}, f32[2,2,128,128]{3,2,1,0:T(8,128)S(1)}, u32[]{:S(2)}, u32[]{:S(2)}) %collective-permute-start.3) | collective-permute-done | bytes 262176 | tf_op jit(solution)/shard_map/ppermute | solution.py:114
  92.0 0.7 fusion.2
  92.7 0.7 reduce_sum.9
  94.1 266.7 %all-reduce.5.cloned.1.call-done = f32[2,128,128]{2,1,0:T(8,128)} async-done(((f32[2,128,128]{2,1,0:T(8,128)}), f32[2,128,128]{2,1,0:T(8,128)}) %all-reduce.5.cloned.1.call-update) | async-done | bytes 131088 | tf_op jit(solution)/shard_map/psum | solution.py:141
  360.7 1.6 broadcast_divide_fusion
  362.3 32.0 %all-reduce.3.cloned.1.call-done = f32[2,2,1024,128]{3,2,1,0:T(8,128)} async-done(((f32[2,2,1024,128]{3,2,1,0:T(8,128)}), f32[2,2,1024,128]{3,2,1,0:T(8,128)}) %all-reduce.3.cloned.1.call-update) | async-done | bytes 2097168 | tf_op jit(solution)/shard_map/psum | solution.py:139
  394.3 1.7 slice_bitcast_fusion.2
  395.9 1.5 pad_maximum_fusion.1
  (17 shorter events, 0.1 us)
Async XLA Ops:
  7.2 27.1 %slice-start = ((f32[2,1024,256]{2,1,0:T(8,128)}), f32[2,128,256]{2,1,0:T(8,128)S(1)}, s32[]{:S(2)}) async-start(f32[2,1024,256]{2,1,0:T(8,128)} %param.12), calls=%async_computation.2 | async-start | bytes 524288 | tf_op jit(solution)/shard_map/slice | solution.py:124
  7.2 29.2 %copy-start.6 = (s32[8,16]{1,0:T(8,128)S(1)}, s32[8,16]{1,0:T(8,128)}, u32[]{:S(2)}) copy-start(s32[8,16]{1,0:T(8,128)} %param.17) | copy-start | bytes 1540
  7.2 353.6 %all-reduce.5.cloned.1.call-start = ((), (), s32[]{:S(2)}) async-start(), calls=%async_computation.1 | async-start | bytes 262144 | tf_op jit(solution)/shard_map/psum | solution.py:141
  9.0 25.3 %collective-permute-start = (f32[2,1024,128]{2,1,0:T(8,128)S(1)}, f32[2,1024,128]{2,1,0:T(8,128)S(1)}, u32[]{:S(2)}, u32[]{:S(2)}) collective-permute-start(f32[2,1024,128]{2,1,0:T(8,128)S(1)} %get-tuple-element.33), channel_id=1, source_target_pairs={{2,0},{4,2},{6,4},{8,6},{10,8},{12,10},{14,12},{16,14},{18,16},{20... | collective-permute-start | bytes 3145736 | tf_op jit(solution)/shard_map/ppermute | solution.py:114
  35.1 18.4 %collective-permute-start.1 = (f32[2,128,384]{2,1,0:T(8,128)}, f32[2,128,384]{2,1,0:T(8,128)}, u32[]{:S(2)}, u32[]{:S(2)}) collective-permute-start(f32[2,128,384]{2,1,0:T(8,128)} %pad_maximum_fusion.2), channel_id=1, source_target_pairs={{32,0},{64,32},{96,64},{128,96},{160,128},{192,160},{224,192},{33,... | collective-permute-start | bytes 1179656 | tf_op jit(solution)/shard_map/ppermute | solution.py:114
  54.8 2.2 copy-start
  54.8 2.2 copy-start.1
  54.8 2.3 copy-start.2
  54.9 2.4 copy-start.3
  54.9 2.4 copy-start.4
  54.9 2.4 copy-start.5
  60.2 24.2 %collective-permute-start.2 = (f32[2,1152,128]{2,1,0:T(8,128)S(1)}, f32[2,1152,128]{2,1,0:T(8,128)S(1)}, u32[]{:S(2)}, u32[]{:S(2)}) collective-permute-start(f32[2,1152,128]{2,1,0:T(8,128)S(1)} %slice_bitcast_fusion), channel_id=1, source_target_pairs={{0,2},{2,4},{4,6},{6,8},{8,10},{10,12},{12,14},{14,16},{16,18},{18... | collective-permute-start | bytes 3538952 | tf_op jit(solution)/shard_map/ppermute | solution.py:114
  84.6 7.4 %collective-permute-start.3 = (f32[2,2,128,128]{3,2,1,0:T(8,128)S(1)}, f32[2,2,128,128]{3,2,1,0:T(8,128)S(1)}, u32[]{:S(2)}, u32[]{:S(2)}) collective-permute-start(f32[2,2,128,128]{3,2,1,0:T(8,128)S(1)} %slice.120), channel_id=1, source_target_pairs={{0,32},{32,64},{64,96},{96,128},{128,160},{160,192},{192,224},{1,3... | collective-permute-start | bytes 786440 | tf_op jit(solution)/shard_map/ppermute | solution.py:114
  85.9 308.3 %all-reduce.3.cloned.1.call-start = ((), (), s32[]{:S(2)}) async-start(), calls=%async_computation | async-start | bytes 4194304 | tf_op jit(solution)/shard_map/psum | solution.py:139
Sparse Core Ops, SparseCore 0:
  86.0 274.6 all-reduce.4
  363.9 30.3 all-reduce.2

commit v2 on v1

--- a/solution.py
+++ b/solution.py
@@ -13,6 +13,248 @@
 BLK = 8
 
 N = 128
+LEVELS = 32766.0
+MESH = pl.DeviceIdType.MESH
+
+
+def encode(x):
+    rows = x.shape[0]
+    tiles = x.reshape(rows // 8, 8, N)
+    peak = jnp.max(jnp.abs(tiles), axis=0)
+    scaled = tiles * (LEVELS / jnp.maximum(peak, 1e-30))[None]
+    return jnp.round(scaled.reshape(rows, N)).astype(jnp.int32).astype(jnp.int16), peak * (1.0 / LEVELS)
+
+
+def decode(code, step):
+    rows = code.shape[0]
+    value = code.astype(jnp.int32).astype(jnp.float32)
+    return (value.reshape(rows // 8, 8, N) * step[None]).reshape(rows, N)
+
+
+def remote(src, dst, send_sem, recv_sem, where):
+    return pltpu.make_async_remote_copy(
+        src_ref=src, dst_ref=dst, send_sem=send_sem, recv_sem=recv_sem, device_id=where, device_id_type=MESH)
+
+
+def collect_kernel(nty, ntx, counts_ref, acc_ref, pg_ref, out_ref, pgo_ref,
+                   theirs, pg_theirs, code_out, step_out, code_in, step_in, by_ty, by_tx, part,
+                   pair_send, pair_recv, strip_send, strip_recv, ty_send, ty_recv, tx_send, tx_recv, all_send, all_recv):
+    ty, tx, me = lax.axis_index("ty"), lax.axis_index("tx"), lax.axis_index("pa")
+    other = 1 - me
+    height = out_ref.shape[1]
+    nq = out_ref.shape[2] // N
+    peer = {"pa": other}
+    chunk = N // nty
+    sizes = (height, nq * N, N)
+    offs = (0, height, height + nq * N)
+    targets = ({"tx": lax.rem(tx + 1, ntx)}, {"ty": lax.rem(ty + 1, nty)},
+               {"tx": lax.rem(tx + 1, ntx), "ty": lax.rem(ty + 1, nty)})
+    sources = ({"tx": lax.rem(tx + ntx - 1, ntx)}, {"ty": lax.rem(ty + nty - 1, nty)},
+               {"tx": lax.rem(tx + ntx - 1, ntx), "ty": lax.rem(ty + nty - 1, nty)})
+    sends = (tx < ntx - 1, ty < nty - 1, jnp.logical_and(tx < ntx - 1, ty < nty - 1))
+    gets = (tx > 0, ty > 0, jnp.logical_and(tx > 0, ty > 0))
+
+    barrier = pltpu.get_barrier_semaphore()
+    pl.semaphore_signal(barrier, inc=1, device_id=peer, device_id_type=MESH)
+    pl.semaphore_signal(barrier, inc=1, device_id=targets[2], device_id_type=MESH)
+    pl.semaphore_signal(barrier, inc=1, device_id=sources[2], device_id_type=MESH)
+
+    @pl.loop(1, nty)
+    def _(k):
+        pl.semaphore_signal(barrier, inc=1, device_id={"ty": lax.rem(ty + k, nty)}, device_id_type=MESH)
+
+    @pl.loop(1, ntx)
+    def _(k):
+        pl.semaphore_signal(barrier, inc=1, device_id={"tx": lax.rem(tx + k, ntx)}, device_id_type=MESH)
+
+    total = jnp.sum(jnp.sum(counts_ref[...].astype(jnp.float32), axis=1, keepdims=True), axis=0, keepdims=True)
+    pl.semaphore_wait(barrier, 1 + 2 + nty - 1 + ntx - 1)
+
+    def swap(n, src, dst):
+        return remote(src, dst, pair_send.at[n], pair_recv.at[n], peer)
+
+    right = swap(0, acc_ref.at[other, nq], theirs.at[nq])
+    low = [swap(1 + q, acc_ref.at[other, q, pl.ds(height, N)], theirs.at[q, pl.ds(height, N)]) for q in range(nq)]
+    probe_swap = swap(1 + nq, pg_ref.at[other], pg_theirs)
+    body = [swap(2 + nq + q, acc_ref.at[other, q, pl.ds(0, height)], theirs.at[q, pl.ds(0, height)]) for q in range(nq)]
+    right.start()
+    for c in low:
+        c.start()
+    probe_swap.start()
+    for c in reversed(body):
+        c.start()
+
+    def strip(n):
+        size, off = sizes[n], offs[n]
+        return (remote(code_out.at[pl.ds(off, size)], code_in.at[pl.ds(off, size)],
+                       strip_send.at[2 * n], strip_recv.at[2 * n], targets[n]),
+                remote(step_out.at[n], step_in.at[n], strip_send.at[2 * n + 1], strip_recv.at[2 * n + 1], targets[n]))
+
+    def pack(n, value):
+        code_out[pl.ds(offs[n], sizes[n])], step_out[n] = encode(value)
+
+        @pl.when(sends[n])
+        def _():
+            for c in strip(n):
+                c.start()
+
+    right.wait()
+    pack(0, acc_ref[me, nq, :height] + theirs[nq, :height])
+    for c in low:
+        c.wait()
+    pack(1, jnp.concatenate([acc_ref[me, q, height:] + theirs[q, height:] for q in range(nq)], axis=0))
+    pack(2, acc_ref[me, nq, height:] + theirs[nq, height:])
+
+    probe_swap.wait()
+    part[...] = pg_ref[me] + pg_theirs[...]
+
+    def ty_copy(k):
+        return remote(part.at[pl.ds(pl.multiple_of(k * chunk, chunk), chunk)], by_ty.at[ty], ty_send.at[k], ty_recv.at[ty], {"ty": k})
+
+    def ty_arrival(k):
+        return remote(part.at[pl.ds(0, chunk)], by_ty.at[k], ty_send.at[k], ty_recv.at[k], {"ty": k})
+
+    @pl.loop(1, nty)
+    def _(k):
+        ty_copy(lax.rem(ty + k, nty)).start()
+
+    by_ty[ty] = part[pl.ds(pl.multiple_of(ty * chunk, chunk), chunk)]
+
+    for q in reversed(range(nq)):
+        body[q].wait()
+        out_ref[me, :, q * N:(q + 1) * N] = acc_ref[me, q, :height] + theirs[q, :height]
+
+    early = [remote(out_ref.at[me, pl.ds(N, height - N), pl.ds(N, (nq - 1) * N)], out_ref.at[me, pl.ds(N, height - N), pl.ds(N, (nq - 1) * N)],
+                    pair_send.at[2 + 2 * nq], pair_recv.at[2 + 2 * nq], peer)]
+    early[0].start()
+
+    @pl.loop(1, nty)
+    def _(k):
+        ty_arrival(lax.rem(ty + k, nty)).wait_recv()
+
+    mine = by_ty[0]
+    for k in range(1, nty):
+        mine = mine + by_ty[k]
+    by_tx[tx] = mine
+
+    def tx_copy(k):
+        return remote(by_tx.at[tx], by_tx.at[tx], tx_send.at[k], tx_recv.at[tx], {"tx": k})
+
+    def tx_arrival(k):
+        return remote(by_tx.at[tx], by_tx.at[k], tx_send.at[k], tx_recv.at[k], {"tx": k})
+
+    @pl.loop(1, ntx)
+    def _(k):
+        tx_copy(lax.rem(tx + k, ntx)).start()
+
+    @pl.when(gets[1])
+    def _():
+        for c in strip(1):
+            c.wait_recv()
+        for q in range(nq):
+            out_ref[me, :N, q * N:(q + 1) * N] += decode(code_in[pl.ds(offs[1] + q * N, N)], step_in[1])
+
+    @pl.when(gets[2])
+    def _():
+        for c in strip(2):
+            c.wait_recv()
+        out_ref[me, :N, :N] += decode(code_in[pl.ds(offs[2], N)], step_in[2])
+
+    @pl.when(gets[0])
+    def _():
+        for c in strip(0):
+            c.wait_recv()
+        out_ref[me, :, :N] += decode(code_in[pl.ds(0, height)], step_in[0])
+
+    late = [remote(out_ref.at[me, :, pl.ds(0, N)], out_ref.at[me, :, pl.ds(0, N)],
+                   pair_send.at[3 + 2 * nq], pair_recv.at[3 + 2 * nq], peer),
+            remote(out_ref.at[me, pl.ds(0, N), pl.ds(N, (nq - 1) * N)], out_ref.at[me, pl.ds(0, N), pl.ds(N, (nq - 1) * N)],
+                   pair_send.at[4 + 2 * nq], pair_recv.at[4 + 2 * nq], peer)]
+    for c in late:
+        c.start()
+
+    @pl.loop(1, ntx)
+    def _(k):
+        tx_arrival(lax.rem(tx + k, ntx)).wait_recv()
+
+    mine = by_tx[0]
+    for k in range(1, ntx):
+        mine = mine + by_tx[k]
+    pgo_ref[me, pl.ds(pl.multiple_of(ty * chunk, chunk), chunk)] = mine / total
+
+    def all_copy(k, at):
+        place = pgo_ref.at[me, pl.ds(pl.multiple_of(at * chunk, chunk), chunk)]
+        return remote(place, place, all_send.at[k], all_recv.at[at], {"ty": k})
+
+    @pl.loop(1, nty)
+    def _(k):
+        all_copy(lax.rem(ty + k, nty), ty).start()
+
+    @pl.loop(1, nty)
+    def _(k):
+        at = lax.rem(ty + k, nty)
+        all_copy(at, at).wait_recv()
+
+    last = swap(5 + 2 * nq, pgo_ref.at[me], pgo_ref.at[me])
+    last.start()
+
+    for n in range(3):
+        @pl.when(sends[n])
+        def _():
+            for c in strip(n):
+                c.wait_send()
+
+    @pl.loop(1, nty)
+    def _(k):
+        at = lax.rem(ty + k, nty)
+        ty_copy(at).wait_send()
+        all_copy(at, ty).wait_send()
+
+    @pl.loop(1, ntx)
+    def _(k):
+        tx_copy(lax.rem(tx + k, ntx)).wait_send()
+
+    for c in early + late:
+        c.wait()
+    last.wait()
+
+
+def collect(counts, acc, pg, height, width):
+    nty, ntx = lax.axis_size("ty"), lax.axis_size("tx")
+    nq = width // N
+    rows = height + nq * N + N
+    chunk = N // nty
+    vmem = pl.BlockSpec(memory_space=pltpu.VMEM)
+    return pl.pallas_call(
+        functools.partial(collect_kernel, nty, ntx),
+        out_shape=(jax.ShapeDtypeStruct((2, height, width), jnp.float32), jax.ShapeDtypeStruct((2, N, N), jnp.float32)),
+        in_specs=[vmem] * 3,
+        out_specs=(vmem, vmem),
+        scratch_shapes=[
+            pltpu.VMEM((nq + 1, height + N, N), jnp.float32),
+            pltpu.VMEM((N, N), jnp.float32),
+            pltpu.VMEM((rows, N), jnp.int16),
+            pltpu.VMEM((3, 8, N), jnp.float32),
+            pltpu.VMEM((rows, N), jnp.int16),
+            pltpu.VMEM((3, 8, N), jnp.float32),
+            pltpu.VMEM((nty, chunk, N), jnp.float32),
+            pltpu.VMEM((ntx, chunk, N), jnp.float32),
+            pltpu.VMEM((N, N), jnp.float32),
+            pltpu.SemaphoreType.DMA((6 + 2 * nq,)),
+            pltpu.SemaphoreType.DMA((6 + 2 * nq,)),
+            pltpu.SemaphoreType.DMA((6,)),
+            pltpu.SemaphoreType.DMA((6,)),
+            pltpu.SemaphoreType.DMA((nty,)),
+            pltpu.SemaphoreType.DMA((nty,)),
+            pltpu.SemaphoreType.DMA((ntx,)),
+            pltpu.SemaphoreType.DMA((ntx,)),
+            pltpu.SemaphoreType.DMA((nty,)),
+            pltpu.SemaphoreType.DMA((nty,)),
+        ],
+        compiler_params=pltpu.CompilerParams(collective_id=1, has_side_effects=True, vmem_limit_bytes=40 << 20),
+        name="collect",
+    )(counts, acc, pg)
+
 
 def dft_tables(length):
     freqs = np.arange(length)
@@ -132,14 +374,7 @@
     grad, probe_part = patches(
         start_row[0, 0], start_col[0, 0], nvalid[None], extended, probe_field, amplitudes[0, 0],
         jnp.asarray(forward), jnp.asarray(inverse), BLK)
-    arrived = from_behind(grad[:, -1], "tx", 1)
-    grad = grad[:, :-1].at[:, 0].add(arrived)
-    arrived_below = from_behind(grad[:, :, height:], "ty", 1)
-    tile = grad[:, :, :height].at[:, :, :N].add(arrived_below)
-    tile = lax.psum(tile, "pa")
-    object_grad = jnp.concatenate([tile[:, q] for q in range(width // N)], axis=2)
-    probe_total = lax.psum(probe_part, ("ty", "tx", "pa"))
-    return object_grad, probe_total / jnp.sum(counts).astype(jnp.float32)
+    return collect(counts, grad, probe_part, height, width)
 
 
 def solution(mesh):

time: 405 us -> 118 us (0.29)
  waiting for transfers between devices: 356 us -> 39.8 us
  Pallas kernels: 2.91 us -> 65.7 us
  between operations: 15.5 us -> 1.44 us
  starting transfers between devices: 15.1 us -> 2.57 us
  other arithmetic: 7.65 us -> 2.99 us
    psum x2 -> x0, waiting for transfers between devices: 299 us -> none  [the longest x1 267 us: shards(): probe_total = lax.psum(probe_part, ('ty', 'tx', 'pa'))]
    pallas_call x0 -> x1, Pallas kernels: none -> 59 us  [collect(): pl.pallas_call(functools.partial(collect_kernel, nty, ntx), out_shape=(ja...]
    ppermute x4 -> x2, waiting for transfers between devices: 57.3 us -> 39.8 us  [from_behind(): lax.ppermute(value, axis, [(source, source + steps) for source in range(i...]
    ppermute x4 -> x2, starting transfers between devices: 15 us -> 2.57 us  [from_behind(): lax.ppermute(value, axis, [(source, source + steps) for source in range(i...]
  transfers between devices with their start and end apart: 6 -> 2, of which waited for: 6 -> 2; matrix products, arithmetic and copies ran while one was open for 1% -> 0% of each run, Pallas kernels for 0% -> 0%
where the time goes in v2:
time: 118 us; the launch traced here: 117 us
  Pallas kernels  65.7 us (56%)
  waiting for transfers between devices  39.8 us (34%)
  local copies, waits for them, and re-layouts  4.99 us (4%)
  other arithmetic  2.99 us (3%)
  starting transfers between devices  2.57 us (2%)
  between operations  1.44 us (1%)
    pallas_call x1, Pallas kernels, collect(): pl.pallas_call(functools.partial(collect_kernel, nty, ntx), out_shape=(ja...  59 us
    ppermute x2, waiting for transfers between devices, from_behind(): lax.ppermute(value, axis, [(source, source + steps) for source in range(i...  39.8 us
    pallas_call x1, Pallas kernels, patches(): pl.pallas_call(functools.partial(patch_kernel, B), out_shape=(jax.ShapeDt...  6.71 us
    unnamed x16, local copies, waits for them, and re-layouts  2.64 us
    ppermute x2, starting transfers between devices, from_behind(): lax.ppermute(value, axis, [(source, source + steps) for source in range(i...  2.57 us
  transfers between devices with their start and end apart: 2, of which 2 were waited for; matrix products, arithmetic and copies ran while one was open for 0% of the time, Pallas kernels for 0%

profile of v2, /device:TPU:1, one launch (start us, length us, event | category | flops | bytes accessed | tf_op | source)
XLA Modules:
  0.0 117.5 jit_solution(5583331576614436763)
XLA Ops:
  0.6 0.0 slice-start
  0.6 1.7 %fusion = (f32[2,1024,128]{2,1,0:T(8,128)S(1)}, f32[2,1024,128]{2,1,0:T(8,128)S(1)}) fusion(f32[2,1024,256]{2,1,0:T(8,128)} %param.8), kind=kLoop, calls=%fused_computation.5 | loop fusion | bytes 4194304 | tf_op jit(solution)/shard_map/slice | solution.py:368
  2.4 0.0 copy-start.4
  2.4 1.3 %collective-permute-start = (f32[2,1024,128]{2,1,0:T(8,128)S(1)}, f32[2,1024,128]{2,1,0:T(8,128)S(1)}, u32[]{:S(2)}, u32[]{:S(2)}) collective-permute-start(f32[2,1024,128]{2,1,0:T(8,128)S(1)} %get-tuple-element.7), channel_id=1, source_target_pairs={{2,0},{4,2},{6,4},{8,6},{10,8},{12,10},{14,12},{16,14},{18,16},{20... | collective-permute-start | bytes 3145736 | tf_op jit(solution)/shard_map/ppermute | solution.py:356
  3.7 24.0 %collective-permute-done = f32[2,1024,128]{2,1,0:T(8,128)S(1)} collective-permute-done((f32[2,1024,128]{2,1,0:T(8,128)S(1)}, f32[2,1024,128]{2,1,0:T(8,128)S(1)}, u32[]{:S(2)}, u32[]{:S(2)}) %collective-permute-start) | collective-permute-done | bytes 1048608 | tf_op jit(solution)/shard_map/ppermute | solution.py:356
  27.7 0.0 slice-done
  27.7 0.8 pad_maximum_fusion.1
  28.5 1.3 %collective-permute-start.1 = (f32[2,128,384]{2,1,0:T(8,128)}, f32[2,128,384]{2,1,0:T(8,128)S(1)}, u32[]{:S(2)}, u32[]{:S(2)}) collective-permute-start(f32[2,128,384]{2,1,0:T(8,128)} %pad_maximum_fusion.1), channel_id=1, source_target_pairs={{32,0},{64,32},{96,64},{128,96},{160,128},{192,160},{224,192},{33,... | collective-permute-start | bytes 1179656 | tf_op jit(solution)/shard_map/ppermute | solution.py:356
  29.8 0.0 copy-done.4
  29.8 0.6 dynamic_slice.3
  31.1 15.8 %collective-permute-done.1 = f32[2,128,384]{2,1,0:T(8,128)S(1)} collective-permute-done((f32[2,128,384]{2,1,0:T(8,128)}, f32[2,128,384]{2,1,0:T(8,128)S(1)}, u32[]{:S(2)}, u32[]{:S(2)}) %collective-permute-start.1) | collective-permute-done | bytes 393248 | tf_op jit(solution)/shard_map/ppermute | solution.py:356
  46.9 0.2 maximum_bitcast_fusion
  47.0 0.1 maximum_bitcast_fusion.2
  47.1 0.0 copy-start
  47.1 0.0 copy-start.1
  47.1 0.0 copy-start.2
  47.1 0.0 copy-start.3
  47.2 0.0 copy-start.5
  47.2 0.0 copy-start.6
  47.2 2.0 %pad_maximum_fusion.ext_ref = f32[2,3,1152,128]{3,2,1,0:T(8,128)} fusion(f32[2,1,1152,128]{3,2,1,0:T(8,128)S(1)} %maximum_bitcast_fusion.2, f32[2,1,1152,128]{3,2,1,0:T(8,128)S(1)} %get-tuple-element.12, f32[2,1,1152,128]{3,2,1,0:T(8,128)S(1)} %get-tuple-element.11), kind=kLoop, calls=%fused_computation | loop fusion | flops 1769472 | bytes 7077888 | tf_op jit(solution)/shard_map/stack | solution.py:369
  49.2 0.3 copy-done
  49.5 0.0 copy-done.1
  49.5 0.1 copy-done.2
  49.7 0.1 copy-done.3
  49.8 0.0 copy-done.5
  49.8 0.0 copy-done.6
  49.8 6.7 %patches.1 = (f32[2,3,1152,128]{3,2,1,0:T(8,128)S(1)}, f32[2,128,128]{2,1,0:T(8,128)S(1)}) custom-call(s32[64]{0:T(128)S(1)} %bitcast.14, s32[64]{0:T(128)S(1)} %bitcast.15, s32[1]{0:T(128)} %bitcast.3.lim_ref, f32[2,3,1152,128]{3,2,1,0:T(8,128)} %pad_maximum_fusion.ext_ref, f32[2,128,128]{2,1,0:T(8,128)S(1)} %copy-done.1, ...), custom_call_target="tpu_custom_call" | custom-call | tf_op jit(solution)/shard_map/patches/pallas_call | solution.py:342
  56.5 59.0 %collect.1 = (f32[2,1024,256]{2,1,0:T(8,128)S(1)}, f32[2,128,128]{2,1,0:T(8,128)S(1)}) custom-call(s32[8,16]{1,0:T(8,128)S(1)} %copy-done.4, f32[2,3,1152,128]{3,2,1,0:T(8,128)S(1)} %get-tuple-element.4.acc_ref, f32[2,128,128]{2,1,0:T(8,128)S(1)} %get-tuple-element.5.pg_ref), custom_call_target="tpu_custom_call" | custom-call | tf_op jit(solution)/shard_map/collect/pallas_call | solution.py:228
  115.5 1.3 %copy.13 = f32[2,1024,256]{2,1,0:T(8,128)} copy(f32[2,1024,256]{2,1,0:T(8,128)S(1)} %get-tuple-element.15) | data formatting | bytes 4194304
  116.8 0.7 copy.14
  (2 shorter events, 0.0 us)
Async XLA Ops:
  0.6 27.1 %slice-start = ((f32[2,1024,256]{2,1,0:T(8,128)}), f32[2,128,256]{2,1,0:T(8,128)S(1)}, s32[]{:S(2)}) async-start(f32[2,1024,256]{2,1,0:T(8,128)} %param.8), calls=%async_computation | async-start | bytes 524288 | tf_op jit(solution)/shard_map/slice | solution.py:366
  2.4 27.4 %copy-start.4 = (s32[8,16]{1,0:T(8,128)S(1)}, s32[8,16]{1,0:T(8,128)}, u32[]{:S(2)}) copy-start(s32[8,16]{1,0:T(8,128)} %counts_ref.1) | copy-start | bytes 1540
  2.4 25.3 %collective-permute-start = (f32[2,1024,128]{2,1,0:T(8,128)S(1)}, f32[2,1024,128]{2,1,0:T(8,128)S(1)}, u32[]{:S(2)}, u32[]{:S(2)}) collective-permute-start(f32[2,1024,128]{2,1,0:T(8,128)S(1)} %get-tuple-element.7), channel_id=1, source_target_pairs={{2,0},{4,2},{6,4},{8,6},{10,8},{12,10},{14,12},{16,14},{18,16},{20... | collective-permute-start | bytes 3145736 | tf_op jit(solution)/shard_map/ppermute | solution.py:356
  28.5 18.3 %collective-permute-start.1 = (f32[2,128,384]{2,1,0:T(8,128)}, f32[2,128,384]{2,1,0:T(8,128)S(1)}, u32[]{:S(2)}, u32[]{:S(2)}) collective-permute-start(f32[2,128,384]{2,1,0:T(8,128)} %pad_maximum_fusion.1), channel_id=1, source_target_pairs={{32,0},{64,32},{96,64},{128,96},{160,128},{192,160},{224,192},{33,... | collective-permute-start | bytes 1179656 | tf_op jit(solution)/shard_map/ppermute | solution.py:356
  47.1 2.4 %copy-start = (bf16[1,1,64,128,128]{4,3,2,1,0:T(8,128)(2,1)S(1)}, bf16[1,1,64,128,128]{4,3,2,1,0:T(8,128)(2,1)}, u32[]{:S(2)}) copy-start(bf16[1,1,64,128,128]{4,3,2,1,0:T(8,128)(2,1)} %param.10) | copy-start | bytes 6291460
  47.1 2.4 %copy-start.1 = (f32[2,128,128]{2,1,0:T(8,128)S(1)}, f32[2,128,128]{2,1,0:T(8,128)}, u32[]{:S(2)}) copy-start(f32[2,128,128]{2,1,0:T(8,128)} %probe_ref.1) | copy-start | bytes 393220
  47.1 2.5 %copy-start.2 = (bf16[256,256]{1,0:T(8,128)(2,1)S(1)}, bf16[256,256]{1,0:T(8,128)(2,1)}, u32[]{:S(2)}) copy-start(bf16[256,256]{1,0:T(8,128)(2,1)} %constant.27.clone.inv_ref) | copy-start | bytes 393220
  47.1 2.6 %copy-start.3 = (bf16[256,256]{1,0:T(8,128)(2,1)S(1)}, bf16[256,256]{1,0:T(8,128)(2,1)}, u32[]{:S(2)}) copy-start(bf16[256,256]{1,0:T(8,128)(2,1)} %constant.26.clone.fwd_ref) | copy-start | bytes 393220
  47.2 2.6 %copy-start.5 = (s32[1,1,64]{2,1,0:T(1,128)S(1)}, s32[1,1,64]{2,1,0:T(1,128)}, u32[]{:S(2)}) copy-start(s32[1,1,64]{2,1,0:T(1,128)} %param.11) | copy-start | bytes 772
  47.2 2.6 %copy-start.6 = (s32[1,1,64]{2,1,0:T(1,128)S(1)}, s32[1,1,64]{2,1,0:T(1,128)}, u32[]{:S(2)}) copy-start(s32[1,1,64]{2,1,0:T(1,128)} %param.12) | copy-start | bytes 772

commit v3 on v2

v3 whole, which is shorter than its diff:
```python
import functools
import math

import jax
import jax.numpy as jnp
import ml_dtypes
import numpy as np
from jax import lax
from jax.experimental import pallas as pl
from jax.experimental.pallas import tpu as pltpu
from jax.sharding import PartitionSpec as P

BLK = 8

N = 128
LEVELS = 32766.0
MESH = pl.DeviceIdType.MESH


def encode(x):
    rows = x.shape[0]
    tiles = x.reshape(rows // 8, 8, N)
    peak = jnp.max(jnp.abs(tiles), axis=0)
    scaled = tiles * (LEVELS / jnp.maximum(peak, 1e-30))[None]
    return jnp.round(scaled.reshape(rows, N)).astype(jnp.int32).astype(jnp.int16), peak * (1.0 / LEVELS)


def decode(code, step):
    rows = code.shape[0]
    value = code.astype(jnp.int32).astype(jnp.float32)
    return (value.reshape(rows // 8, 8, N) * step[None]).reshape(rows, N)


def remote(src, dst, send_sem, recv_sem, where):
    return pltpu.make_async_remote_copy(
        src_ref=src, dst_ref=dst, send_sem=send_sem, recv_sem=recv_sem, device_id=where, device_id_type=MESH)


def collect_kernel(nty, ntx, zh, zl, counts_ref, acc_ref, pg_ref, out_ref, pgo_ref,
                   theirs, pg_theirs, code_out, step_out, code_in, step_in, by_line, by_plane, part,
                   pair_send, pair_recv, strip_send, strip_recv, line_send, line_recv, plane_send, plane_recv, all_send, all_recv):
    ty, tx, me = lax.axis_index("ty"), lax.axis_index("tx"), lax.axis_index("pa")
    other = 1 - me
    height = out_ref.shape[1]
    nq = out_ref.shape[2] // N
    peer = {"pa": other}
    nline, nplane = zh * zl, (nty // zh) * (ntx // zl)
    chunk = N // nline
    line_id = lax.rem(ty, zh) * zl + lax.rem(tx, zl)
    plane_id = (ty // zh) * (ntx // zl) + tx // zl

    def in_line(k):
        return {"ty": (ty // zh) * zh + k // zl, "tx": (tx // zl) * zl + lax.rem(k, zl)}

    def in_plane(k):
        return {"ty": (k // (ntx // zl)) * zh + lax.rem(ty, zh), "tx": lax.rem(k, ntx // zl) * zl + lax.rem(tx, zl)}

    def next_in_line(k):
        return lax.rem(line_id + k, nline)

    def next_in_plane(k):
        return lax.rem(plane_id + k, nplane)

    sizes = (height, nq * N, N)
    offs = (0, height, height + nq * N)
    targets = ({"tx": lax.rem(tx + 1, ntx)}, {"ty": lax.rem(ty + 1, nty)},
               {"tx": lax.rem(tx + 1, ntx), "ty": lax.rem(ty + 1, nty)})
    sources = ({"tx": lax.rem(tx + ntx - 1, ntx)}, {"ty": lax.rem(ty + nty - 1, nty)},
               {"tx": lax.rem(tx + ntx - 1, ntx), "ty": lax.rem(ty + nty - 1, nty)})
    sends = (tx < ntx - 1, ty < nty - 1, jnp.logical_and(tx < ntx - 1, ty < nty - 1))
    gets = (tx > 0, ty > 0, jnp.logical_and(tx > 0, ty > 0))

    barrier = pltpu.get_barrier_semaphore()
    for where in (peer,) + targets + sources:
        pl.semaphore_signal(barrier, inc=1, device_id=where, device_id_type=MESH)

    @pl.loop(1, nline)
    def _(k):
        pl.semaphore_signal(barrier, inc=1, device_id=in_line(next_in_line(k)), device_id_type=MESH)

    @pl.loop(1, nplane)
    def _(k):
        pl.semaphore_signal(barrier, inc=1, device_id=in_plane(next_in_plane(k)), device_id_type=MESH)

    total = jnp.sum(jnp.sum(counts_ref[...].astype(jnp.float32), axis=1, keepdims=True), axis=0, keepdims=True)
    pl.semaphore_wait(barrier, 1 + 6 + nline - 1 + nplane - 1)

    def swap(n, src, dst):
        return remote(src, dst, pair_send.at[n], pair_recv.at[n], peer)

    probe_swap = swap(1 + nq, pg_ref.at[other], pg_theirs)
    right = swap(0, acc_ref.at[other, nq], theirs.at[nq])
    low = [swap(1 + q, acc_ref.at[other, q, pl.ds(height, N)], theirs.at[q, pl.ds(height, N)]) for q in range(nq)]
    body = [swap(2 + nq + q, acc_ref.at[other, q, pl.ds(0, height)], theirs.at[q, pl.ds(0, height)]) for q in range(nq)]
    probe_swap.start()
    for c in low:
        c.start()
    right.start()
    for c in reversed(body):
        c.start()

    def strip(n):
        size, off = sizes[n], offs[n]
        return (remote(code_out.at[pl.ds(off, size)], code_in.at[pl.ds(off, size)],
                       strip_send.at[2 * n], strip_recv.at[2 * n], targets[n]),
                remote(step_out.at[n], step_in.at[n], strip_send.at[2 * n + 1], strip_recv.at[2 * n + 1], targets[n]))

    def pack(n, value):
        code_out[pl.ds(offs[n], sizes[n])], step_out[n] = encode(value)

        @pl.when(sends[n])
        def _():
            for c in strip(n):
                c.start()

    def rows_of(k):
        return pl.ds(pl.multiple_of(k * chunk, chunk), chunk)

    def line_copy(k):
        return remote(part.at[rows_of(k)], by_line.at[line_id], line_send.at[k], line_recv.at[line_id], in_line(k))

    def line_arrival(k):
        return remote(part.at[rows_of(k)], by_line.at[k], line_send.at[k], line_recv.at[k], in_line(k))

    def plane_copy(k):
        return remote(by_plane.at[plane_id], by_plane.at[plane_id], plane_send.at[k], plane_recv.at[plane_id], in_plane(k))

    def plane_arrival(k):
        return remote(by_plane.at[plane_id], by_plane.at[k], plane_send.at[k], plane_recv.at[k], in_plane(k))

    def all_copy(k, at):
        place = pgo_ref.at[me, rows_of(at)]
        return remote(place, place, all_send.at[k], all_recv.at[at], in_line(k))

    probe_swap.wait()
    part[...] = pg_ref[me] + pg_theirs[...]

    @pl.loop(1, nline)
    def _(k):
        line_copy(next_in_line(k)).start()

    by_line[line_id] = part[rows_of(line_id)]

    for c in low:
        c.wait()
    pack(1, jnp.concatenate([acc_ref[me, q, height:] + theirs[q, height:] for q in range(nq)], axis=0))
    right.wait()
    pack(2, acc_ref[me, nq, height:] + theirs[nq, height:])
    pack(0, acc_ref[me, nq, :height] + theirs[nq, :height])

    @pl.loop(1, nline)
    def _(k):
        line_arrival(next_in_line(k)).wait_recv()

    mine = by_line[0]
    for k in range(1, nline):
        mine = mine + by_line[k]
    by_plane[plane_id] = mine

    @pl.loop(1, nplane)
    def _(k):
        plane_copy(next_in_plane(k)).start()

    for q in reversed(range(nq)):
        body[q].wait()
        out_ref[me, :, q * N:(q + 1) * N] = acc_ref[me, q, :height] + theirs[q, :height]

    def final(n, rows, columns):
        place = out_ref.at[me, rows, columns]
        return swap(n, place, place)

    rest = pl.ds(N, (nq - 1) * N)
    early = final(2 + 2 * nq, pl.ds(N, height - N), rest)
    early.start()

    @pl.loop(1, nplane)
    def _(k):
        plane_arrival(next_in_plane(k)).wait_recv()

    mine = by_plane[0]
    for k in range(1, nplane):
        mine = mine + by_plane[k]
    pgo_ref[me, rows_of(line_id)] = mine / total

    @pl.loop(1, nline)
    def _(k):
        all_copy(next_in_line(k), line_id).start()

    @pl.when(gets[1])
    def _():
        for c in strip(1):
            c.wait_recv()
        for q in range(nq):
            out_ref[me, :N, q * N:(q + 1) * N] += decode(code_in[pl.ds(offs[1] + q * N, N)], step_in[1])

    @pl.when(gets[2])
    def _():
        for c in strip(2):
            c.wait_recv()
        out_ref[me, :N, :N] += decode(code_in[pl.ds(offs[2], N)], step_in[2])

    @pl.when(gets[0])
    def _():
        for c in strip(0):
            c.wait_recv()
        out_ref[me, :, :N] += decode(code_in[pl.ds(0, height)], step_in[0])

    late = [final(3 + 2 * nq, pl.ds(0, height), pl.ds(0, N)), final(4 + 2 * nq, pl.ds(0, N), rest)]
    for c in late:
        c.start()

    @pl.loop(1, nline)
    def _(k):
        at = next_in_line(k)
        all_copy(at, at).wait_recv()

    last = swap(5 + 2 * nq, pgo_ref.at[me], pgo_ref.at[me])
    last.start()

    for n in range(3):
        @pl.when(sends[n])
        def _():
            for c in strip(n):
                c.wait_send()

    @pl.loop(1, nline)
    def _(k):
        at = next_in_line(k)
        line_copy(at).wait_send()
        all_copy(at, line_id).wait_send()

    @pl.loop(1, nplane)
    def _(k):
        plane_copy(next_in_plane(k)).wait_send()

    early.wait()
    for c in late:
        c.wait()
    last.wait()


def collect(counts, acc, pg, height, width, zh=2, zl=4):
    nty, ntx = lax.axis_size("ty"), lax.axis_size("tx")
    nq = width // N
    rows = height + nq * N + N
    nline, nplane = zh * zl, (nty // zh) * (ntx // zl)
    chunk = N // nline
    vmem = pl.BlockSpec(memory_space=pltpu.VMEM)
    dma = pltpu.SemaphoreType.DMA
    return pl.pallas_call(
        functools.partial(collect_kernel, nty, ntx, zh, zl),
        out_shape=(jax.ShapeDtypeStruct((2, height, width), jnp.float32), jax.ShapeDtypeStruct((2, N, N), jnp.float32)),
        in_specs=[vmem] * 3,
        out_specs=(vmem, vmem),
        scratch_shapes=[
            pltpu.VMEM((nq + 1, height + N, N), jnp.float32),
            pltpu.VMEM((N, N), jnp.float32),
            pltpu.VMEM((rows, N), jnp.int16),
            pltpu.VMEM((3, 8, N), jnp.float32),
            pltpu.VMEM((rows, N), jnp.int16),
            pltpu.VMEM((3, 8, N), jnp.float32),
            pltpu.VMEM((nline, chunk, N), jnp.float32),
            pltpu.VMEM((nplane, chunk, N), jnp.float32),
            pltpu.VMEM((N, N), jnp.float32),
            dma((6 + 2 * nq,)), dma((6 + 2 * nq,)), dma((6,)), dma((6,)),
            dma((nline,)), dma((nline,)), dma((nplane,)), dma((nplane,)), dma((nline,)), dma((nline,)),
        ],
        compiler_params=pltpu.CompilerParams(collective_id=1, has_side_effects=True, vmem_limit_bytes=40 << 20),
        name="collect",
    )(counts, acc, pg)


def spread_kernel(nty, ntx, cuts, obj_ref, amp_ref, rows_ref, cols_ref, ext_ref, shared_ref, list_ref,
                  spots, local_sem, strip_send, strip_recv, pair_send, pair_recv):
    ty, tx, me = lax.axis_index("ty"), lax.axis_index("tx"), lax.axis_index("pa")
    other = 1 - me
    height = obj_ref.shape[1]
    nq = obj_ref.shape[2] // N
    slots = amp_ref.shape[0]
    moved = slots // 2
    peer = {"pa": other}
    up, down = lax.rem(ty + nty - 1, nty), lax.rem(ty + 1, nty)
    left, right = lax.rem(tx + ntx - 1, ntx), lax.rem(tx + 1, ntx)

    barrier = pltpu.get_barrier_semaphore()
    for where in (peer, {"tx": left}, {"tx": right}, {"ty": up}, {"ty": down}, {"tx": left, "ty": up}, {"tx": right, "ty": down}):
        pl.semaphore_signal(barrier, inc=1, device_id=where, device_id_type=MESH)

    local = [pltpu.make_async_copy(obj_ref.at[p, :, pl.ds(q * N, N)], ext_ref.at[p, q, pl.ds(0, height)], local_sem.at[p * nq + q])
             for p in range(2) for q in range(nq)]
    local.append(pltpu.make_async_copy(amp_ref, shared_ref.at[pl.ds(me * moved, slots)], local_sem.at[2 * nq]))
    places = [pltpu.make_async_copy(rows_ref, spots.at[0], local_sem.at[2 * nq + 1]),
              pltpu.make_async_copy(cols_ref, spots.at[1], local_sem.at[2 * nq + 2])]
    for c in places + local:
        c.start()
    for c in places:
        c.wait()
    list_ref[me, 0:1, :slots] = spots[0, 0]
    list_ref[me, 1:2, :slots] = spots[1, 0]

    step = height // cuts
    has_right, has_below = tx < ntx - 1, ty < nty - 1
    gives_left, gives_up = tx > 0, ty > 0
    pieces = [(gives_up, has_below, {"ty": up}, q, height, 0, N, q) for q in range(nq)]
    pieces.append((jnp.logical_and(gives_left, gives_up), jnp.logical_and(has_right, has_below), {"tx": left, "ty": up}, nq, height, 0, N, 0))
    pieces += [(gives_left, has_right, {"tx": left}, nq, k * step, k * step, step, 0) for k in range(cuts)]

    def strip(n):
        _, _, where, q, row, first, size, source = pieces[n]
        return remote(obj_ref.at[me, pl.ds(first, size), pl.ds(source * N, N)], ext_ref.at[me, q, pl.ds(row, size)],
                      strip_send.at[n], strip_recv.at[n], where)

    def forward(n):
        _, _, _, q, row, _, size, _ = pieces[n]
        place = ext_ref.at[me, q, pl.ds(row, size)]
        return remote(place, place, pair_send.at[n], pair_recv.at[n], peer)

    pl.semaphore_wait(barrier, 7)
    for n, piece in enumerate(pieces):
        @pl.when(piece[0])
        def _():
            strip(n).start()

    extra = len(pieces)
    lists = remote(list_ref.at[me], list_ref.at[me], pair_send.at[extra], pair_recv.at[extra], peer)
    lists.start()
    move = remote(amp_ref.at[pl.ds(moved, slots - moved)], shared_ref.at[pl.ds(0, slots - moved)],
                  pair_send.at[extra + 1], pair_recv.at[extra + 1], peer)

    @pl.when(me == 0)
    def _():
        move.start()

    for n, piece in enumerate(pieces):
        @pl.when(jnp.logical_not(piece[1]))
        def _():
            _, _, _, q, row, _, size, _ = piece
            for p in range(2):
                ext_ref[p, q, row:row + size] = jnp.zeros((size, N), jnp.float32)

    order = list(range(nq + 1, len(pieces))) + list(range(nq + 1))
    for n in order:
        @pl.when(pieces[n][1])
        def _():
            strip(n).wait_recv()
            forward(n).start()

    for c in local:
        c.wait()
    lists.wait()

    @pl.when(me == 0)
    def _():
        move.wait_send()

    @pl.when(me == 1)
    def _():
        move.wait_recv()

    for n, piece in enumerate(pieces):
        @pl.when(piece[0])
        def _():
            strip(n).wait_send()

        @pl.when(piece[1])
        def _():
            forward(n).wait()


def spread(obj, amp, rows, cols, cuts=4):
    nty, ntx = lax.axis_size("ty"), lax.axis_size("tx")
    height, width = obj.shape[1:]
    slots = amp.shape[0]
    nq = width // N
    pieces = nq + 1 + cuts
    vmem = pl.BlockSpec(memory_space=pltpu.VMEM)
    hbm = pl.BlockSpec(memory_space=pltpu.HBM)
    dma = pltpu.SemaphoreType.DMA
    return pl.pallas_call(
        functools.partial(spread_kernel, nty, ntx, cuts),
        out_shape=(
            jax.ShapeDtypeStruct((2, nq + 1, height + N, N), jnp.float32),
            jax.ShapeDtypeStruct((slots + slots // 2, N, N), jnp.bfloat16),
            jax.ShapeDtypeStruct((2, 8, N), jnp.int32),
        ),
        in_specs=[hbm] * 4,
        out_specs=(vmem, vmem, vmem),
        scratch_shapes=[
            pltpu.VMEM((2, 1, 1, slots), jnp.int32),
            dma((2 * nq + 3,)), dma((pieces,)), dma((pieces,)), dma((pieces + 2,)), dma((pieces + 2,)),
        ],
        compiler_params=pltpu.CompilerParams(collective_id=0, has_side_effects=True, vmem_limit_bytes=40 << 20),
        name="spread",
    )(obj, amp, rows, cols)


def dft_tables(length):
    freqs = np.arange(length)
    angle = (freqs[:, None] * freqs[None, :] % length) * (2.0 * math.pi / length)
    cosine = np.cos(angle) / math.sqrt(length)
    sine = np.sin(angle) / math.sqrt(length)
    forward = np.block([[cosine, -sine], [sine, cosine]]).astype(ml_dtypes.bfloat16)
    inverse = np.block([[cosine, sine], [-sine, cosine]]).astype(ml_dtypes.bfloat16)
    return forward, inverse

def mm(a, b):
    return jnp.dot(a, b, preferred_element_type=jnp.float32)

def patch_kernel(B, slots, counts_ref, list_ref, ext_ref, probe_ref, amp_ref, fwd_ref, inv_ref,
                 acc_ref, pg_ref, patch_ref):
    acc_ref[...] = jnp.zeros_like(acc_ref)
    pg_ref[...] = jnp.zeros_like(pg_ref)
    lane = lax.broadcasted_iota(jnp.int32, (N, N), 1)
    me = lax.axis_index("pa")
    count = counts_ref[lax.axis_index("ty"), lax.axis_index("tx")]
    moved = slots // 2
    split = jnp.maximum((count + 1) // 2, jnp.minimum(count, moved))
    first = jnp.where(me == 0, 0, split)
    last = jnp.where(me == 0, split, count)

    def body(it, _):
        pos = []
        psis = []
        for b in range(B):
            i = first + it * B + b
            number = jnp.minimum(i, last - 1)
            r = list_ref[number // slots, 0, number % slots]
            c = list_ref[number // slots, 1, number % slots]
            slot = number - me * moved
            j = c // N
            s = c % N
            pos.append((slot, i < last, r, j, s))
            back = (N - s) % N
            high = lane >= s
            parts = []
            for p in range(2):
                v = jnp.where(high, ext_ref[p, j, pl.ds(r, N), :], ext_ref[p, j + 1, pl.ds(r, N), :])
                v = pltpu.roll(v, back, 1)
                patch_ref[b, p] = v
                parts.append(v)
            pre, pim = probe_ref[0], probe_ref[1]
            psi_re = pre * parts[0] - pim * parts[1]
            psi_im = pre * parts[1] + pim * parts[0]
            psis.append(jnp.concatenate([psi_re.astype(jnp.bfloat16), psi_im.astype(jnp.bfloat16)], axis=1))
        half = mm(jnp.concatenate(psis, axis=0), fwd_ref[...]).astype(jnp.bfloat16)
        rhs = jnp.concatenate(
            [jnp.concatenate([half[b * N:(b + 1) * N, q * N:(q + 1) * N] for b in range(B)], axis=1) for q in range(2)], axis=0)
        wave = mm(inv_ref[...], rhs)
        chis = [[], []]
        for b in range(B):
            slot, ok, r, j, s = pos[b]
            wre = wave[:N, b * N:(b + 1) * N]
            wim = wave[N:, b * N:(b + 1) * N]
            level = amp_ref[slot].astype(jnp.float32)
            use = ok.astype(jnp.float32)
            factor = (1.0 - level * lax.rsqrt(wre * wre + wim * wim + 1.0)) * use
            chis[0].append((wre * factor).astype(jnp.bfloat16))
            chis[1].append((wim * factor).astype(jnp.bfloat16))
        rhs2 = jnp.concatenate([jnp.concatenate(chis[q], axis=1) for q in range(2)], axis=0)
        bk = mm(fwd_ref[...], rhs2).astype(jnp.bfloat16)
        lhs = jnp.concatenate([jnp.concatenate([bk[q * N:(q + 1) * N, b * N:(b + 1) * N] for q in range(2)], axis=1) for b in range(B)], axis=0)
        grad = mm(lhs, inv_ref[...])
        tre = pg_ref[0]
        tim = pg_ref[1]
        for b in range(B):
            slot, ok, r, j, s = pos[b]
            gre = grad[b * N:(b + 1) * N, :N]
            gim = grad[b * N:(b + 1) * N, N:]
            pre, pim = probe_ref[0], probe_ref[1]
            qre, qim = patch_ref[b, 0], patch_ref[b, 1]
            tre = tre + (qre * gre + qim * gim)
            tim = tim + (qre * gim - qim * gre)
            obj = (pre * gre + pim * gim, pre * gim - pim * gre)
            high = lane >= s
            for p in range(2):
                o = pltpu.roll(obj[p], s, 1)
                acc_ref[p, j, pl.ds(r, N), :] += jnp.where(high, o, 0.0)
                acc_ref[p, j + 1, pl.ds(r, N), :] += jnp.where(high, 0.0, o)
        pg_ref[0] = tre
        pg_ref[1] = tim
        return 0

    lax.fori_loop(0, (last - first + B - 1) // B, body, 0)

def patches(counts, lists, ext, probe, amp, fwd, inv, B):
    smem = pl.BlockSpec(memory_space=pltpu.SMEM)
    vmem = pl.BlockSpec(memory_space=pltpu.VMEM)
    return pl.pallas_call(
        functools.partial(patch_kernel, B, amp.shape[0] * 2 // 3),
        out_shape=(jax.ShapeDtypeStruct(ext.shape, jnp.float32), jax.ShapeDtypeStruct((2, N, N), jnp.float32)),
        in_specs=[smem] * 2 + [vmem] * 5,
        out_specs=(vmem, vmem),
        scratch_shapes=[pltpu.VMEM((B, 2, N, N), jnp.float32)],
        compiler_params=pltpu.CompilerParams(vmem_limit_bytes=40 << 20),
        name="patches",
    )(counts, lists, ext, probe, amp, fwd, inv)


def shards(object_field, probe_field, amplitudes, start_row, start_col, counts):
    height, width = object_field.shape[1:]
    extended, shared, lists = spread(object_field, amplitudes[0, 0], start_row, start_col)
    forward, inverse = dft_tables(N)
    grad, probe_part = patches(
        counts, lists, extended, probe_field, shared, jnp.asarray(forward), jnp.asarray(inverse), BLK)
    return collect(counts, grad, probe_part, height, width)


def solution(mesh):
    return jax.shard_map(
        shards,
        mesh=mesh,
        in_specs=(
            P(None, "ty", "tx"),
            P(),
            P("ty", "tx", "pa", None, None),
            P("ty", "tx", "pa"),
            P("ty", "tx", "pa"),
            P(),
        ),
        out_specs=(P(None, "ty", "tx"), P()),
        check_vma=False,
    )
```

time: 118 us -> 77.9 us (0.66)
  waiting for transfers between devices: 39.8 us -> 0 us
  Pallas kernels: 65.7 us -> 70.6 us
  other arithmetic: 2.99 us -> 0 us
  starting transfers between devices: 2.57 us -> 0 us
  local copies, waits for them, and re-layouts: 4.99 us -> 6.48 us
    ppermute x2 -> x0, waiting for transfers between devices: 39.8 us -> none  [from_behind(): lax.ppermute(value, axis, [(source, source + steps) for source in range(i...]
    pallas_call x2 -> x3, Pallas kernels: 65.7 us -> 70.6 us  [the longest x1 41.1 us: collect(): pl.pallas_call(functools.partial(collect_kernel, nty, ntx, zh, zl), out_s...]
    unnamed x16 -> x18, local copies, waits for them, and re-layouts: 2.64 us -> 6.48 us
    ppermute x2 -> x0, starting transfers between devices: 2.57 us -> none  [from_behind(): lax.ppermute(value, axis, [(source, source + steps) for source in range(i...]
    another operation x3 -> x0, other arithmetic: 2.21 us -> none  [shards(): jnp.stack([jnp.concatenate([block, below[:, :, q * N:(q + 1) * N]], axis=...]
    slice x5 -> x0, local copies, waits for them, and re-layouts: 1.77 us -> none  [the longest x1 1.73 us: shards(): object_field[:, :, q * N:(q + 1) * N]]
  transfers between devices with their start and end apart: 2 -> 0, of which waited for: 2 -> 0; matrix products, arithmetic and copies ran while one was open for 0% -> 0% of each run, Pallas kernels for 0% -> 0%
where the time goes in v3:
time: 77.9 us; the launch traced here: 77.7 us
  Pallas kernels  70.6 us (91%)
  local copies, waits for them, and re-layouts  6.48 us (8%)
    pallas_call x1, Pallas kernels, collect(): pl.pallas_call(functools.partial(collect_kernel, nty, ntx, zh, zl), out_s...  41.1 us
    pallas_call x1, Pallas kernels, spread(): pl.pallas_call(functools.partial(spread_kernel, nty, ntx, cuts), out_shap...  25.5 us
    unnamed x18, local copies, waits for them, and re-layouts  6.48 us
    pallas_call x1, Pallas kernels, patches(): pl.pallas_call(functools.partial(patch_kernel, B, amp.shape[0] * 2 // 3),...  3.99 us

profile of v3, /device:TPU:1, one launch (start us, length us, event | category | flops | bytes accessed | tf_op | source)
XLA Modules:
  0.0 77.7 jit_solution(12297342924247362429)
XLA Ops:
  0.6 0.0 copy-start
  0.6 1.6 %copy-done = f32[2,1024,256]{2,1,0:T(8,128)S(1)} copy-done((f32[2,1024,256]{2,1,0:T(8,128)S(1)}, f32[2,1024,256]{2,1,0:T(8,128)}, u32[]{:S(2)}) %copy-start) | copy-done | bytes 2097176
  2.2 0.0 copy-start.1
  2.2 1.6 %copy-done.1 = bf16[1,1,64,128,128]{4,3,2,1,0:T(8,128)(2,1)S(1)} copy-done((bf16[1,1,64,128,128]{4,3,2,1,0:T(8,128)(2,1)S(1)}, bf16[1,1,64,128,128]{4,3,2,1,0:T(8,128)(2,1)}, u32[]{:S(2)}) %copy-start.1) | copy-done | bytes 2097176
  3.8 0.0 copy-start.6
  3.8 0.7 copy-done.6
  4.5 0.0 copy-start.7
  4.5 0.7 copy-done.7
  5.1 0.0 copy-start.2
  5.1 0.0 copy-start.3
  5.1 0.0 copy-start.4
  5.1 0.0 copy-start.5
  5.1 25.5 %spread.1 = (f32[2,3,1152,128]{3,2,1,0:T(8,128)S(1)}, bf16[96,128,128]{2,1,0:T(8,128)(2,1)S(1)}, s32[2,8,128]{2,1,0:T(8,128)S(1)}) custom-call(f32[2,1024,256]{2,1,0:T(8,128)S(1)} %copy-done, bf16[64,128,128]{2,1,0:T(8,128)(2,1)S(1)} %bitcast.1, s32[1,1,64]{2,1,0:T(1,128)S(1)} %copy-done.6, s32[1,1,64]{2,1,0:T(1,128)S(1)} %copy-done.7), custom_call_target="tpu_custom_call" | custom-call | tf_op jit(solution)/shard_map/spread/pallas_call | solution.py:379
  30.6 0.0 copy-done.2
  30.6 0.0 copy-done.3
  30.6 0.0 copy-done.4
  30.6 0.0 copy-done.5
  30.7 4.0 %patches.1 = (f32[2,3,1152,128]{3,2,1,0:T(8,128)S(1)}, f32[2,128,128]{2,1,0:T(8,128)S(1)}) custom-call(s32[8,16]{1,0:T(8,128)S(1)} %copy-done.5, s32[2,8,128]{2,1,0:T(8,128)S(1)} %get-tuple-element.7.list_ref, f32[2,3,1152,128]{3,2,1,0:T(8,128)S(1)} %get-tuple-element.8.ext_ref, f32[2,128,128]{2,1,0:T(8,128)S(1)} %copy-done.2, ...), custom_call_target="tpu_custom_call" | custom-call | tf_op jit(solution)/shard_map/patches/pallas_call | solution.py:488
  34.7 41.1 %collect.1 = (f32[2,1024,256]{2,1,0:T(8,128)S(1)}, f32[2,128,128]{2,1,0:T(8,128)S(1)}) custom-call(s32[8,16]{1,0:T(8,128)S(1)} %copy-done.5, f32[2,3,1152,128]{3,2,1,0:T(8,128)S(1)} %get-tuple-element.10.acc_ref, f32[2,128,128]{2,1,0:T(8,128)S(1)} %get-tuple-element.11.pg_ref), custom_call_target="tpu_custom_call" | custom-call | tf_op jit(solution)/shard_map/collect/pallas_call | solution.py:250
  75.8 1.3 %copy.12 = f32[2,1024,256]{2,1,0:T(8,128)} copy(f32[2,1024,256]{2,1,0:T(8,128)S(1)} %get-tuple-element.14) | data formatting | bytes 4194304
  77.1 0.7 copy.13
Async XLA Ops:
  0.6 1.6 %copy-start = (f32[2,1024,256]{2,1,0:T(8,128)S(1)}, f32[2,1024,256]{2,1,0:T(8,128)}, u32[]{:S(2)}) copy-start(f32[2,1024,256]{2,1,0:T(8,128)} %obj_ref.1) | copy-start | bytes 6291460
  2.2 1.6 %copy-start.1 = (bf16[1,1,64,128,128]{4,3,2,1,0:T(8,128)(2,1)S(1)}, bf16[1,1,64,128,128]{4,3,2,1,0:T(8,128)(2,1)}, u32[]{:S(2)}) copy-start(bf16[1,1,64,128,128]{4,3,2,1,0:T(8,128)(2,1)} %param.10) | copy-start | bytes 6291460
  3.8 0.7 copy-start.6
  4.5 0.7 copy-start.7
  5.1 25.5 %copy-start.2 = (f32[2,128,128]{2,1,0:T(8,128)S(1)}, f32[2,128,128]{2,1,0:T(8,128)}, u32[]{:S(2)}) copy-start(f32[2,128,128]{2,1,0:T(8,128)} %probe_ref.1) | copy-start | bytes 393220
  5.1 25.5 %copy-start.3 = (bf16[256,256]{1,0:T(8,128)(2,1)S(1)}, bf16[256,256]{1,0:T(8,128)(2,1)}, u32[]{:S(2)}) copy-start(bf16[256,256]{1,0:T(8,128)(2,1)} %constant.5.clone.inv_ref) | copy-start | bytes 393220
  5.1 25.5 %copy-start.4 = (bf16[256,256]{1,0:T(8,128)(2,1)S(1)}, bf16[256,256]{1,0:T(8,128)(2,1)}, u32[]{:S(2)}) copy-start(bf16[256,256]{1,0:T(8,128)(2,1)} %constant.4.clone.fwd_ref) | copy-start | bytes 393220
  5.1 25.5 %copy-start.5 = (s32[8,16]{1,0:T(8,128)S(1)}, s32[8,16]{1,0:T(8,128)}, u32[]{:S(2)}) copy-start(s32[8,16]{1,0:T(8,128)} %counts_ref.3) | copy-start | bytes 1540

commit v4 on v3

--- a/solution.py
+++ b/solution.py
@@ -270,8 +270,39 @@
     )(counts, acc, pg)
 
 
+WIDE = 524287.0
+SPREAD_VMEM = 40 << 20
+
+
+def encode_wide(x):
+    rows = x.shape[0]
+    tiles = x.reshape(rows // 8, 8, N)
+    peak = jnp.max(jnp.abs(tiles), axis=0)
+    scaled = tiles * (WIDE / jnp.maximum(peak, 1e-30))[None]
+    number = jnp.round(scaled.reshape(rows, N)).astype(jnp.int32)
+    return number, peak * (1.0 / WIDE)
+
+
+def split_wide(number):
+    quarter = number.shape[0] // 4
+    low = number & 15
+    word = -32768
+    for g in range(4):
+        word = word + (low[g * quarter:(g + 1) * quarter] << (4 * g))
+    return (number >> 4).astype(jnp.int16), word.astype(jnp.int16)
+
+
+def decode_wide(high, word, step):
+    rows = high.shape[0]
+    low = word.astype(jnp.int32) + 32768
+    low = jnp.concatenate([(low >> (4 * g)) & 15 for g in range(4)], axis=0)
+    value = ((high.astype(jnp.int32) << 4) + low).astype(jnp.float32)
+    return (value.reshape(rows // 8, 8, N) * step[None]).reshape(rows, N)
+
+
 def spread_kernel(nty, ntx, cuts, obj_ref, amp_ref, rows_ref, cols_ref, ext_ref, shared_ref, list_ref,
-                  spots, local_sem, strip_send, strip_recv, pair_send, pair_recv):
+                  spots, code_out, step_out, code_in, step_in, code_pair, step_pair,
+                  local_sem, strip_send, strip_recv, pair_send, pair_recv):
     ty, tx, me = lax.axis_index("ty"), lax.axis_index("tx"), lax.axis_index("pa")
     other = 1 - me
     height = obj_ref.shape[1]
@@ -286,42 +317,77 @@
     for where in (peer, {"tx": left}, {"tx": right}, {"ty": up}, {"ty": down}, {"tx": left, "ty": up}, {"tx": right, "ty": down}):
         pl.semaphore_signal(barrier, inc=1, device_id=where, device_id_type=MESH)
 
-    local = [pltpu.make_async_copy(obj_ref.at[p, :, pl.ds(q * N, N)], ext_ref.at[p, q, pl.ds(0, height)], local_sem.at[p * nq + q])
-             for p in range(2) for q in range(nq)]
+    def load(p, q):
+        return pltpu.make_async_copy(obj_ref.at[p, :, pl.ds(q * N, N)], ext_ref.at[p, q, pl.ds(0, height)], local_sem.at[p * nq + q])
+
+    mine = [load(me, q) for q in range(nq)]
+    local = [load(other, q) for q in range(nq)]
     local.append(pltpu.make_async_copy(amp_ref, shared_ref.at[pl.ds(me * moved, slots)], local_sem.at[2 * nq]))
     places = [pltpu.make_async_copy(rows_ref, spots.at[0], local_sem.at[2 * nq + 1]),
               pltpu.make_async_copy(cols_ref, spots.at[1], local_sem.at[2 * nq + 2])]
-    for c in places + local:
+    for c in mine + places + local:
         c.start()
+
+    size = height // cuts
+    long, short = size * 5 // 4, N * 5 // 4
+    has_right, has_below = tx < ntx - 1, ty < nty - 1
+    gives_left, gives_up = tx > 0, ty > 0
+    base = cuts * long
+    pieces = [(gives_up, has_below, {"ty": up}, q, height, N, base + q * short, base + q * short, cuts) for q in range(nq)]
+    pieces.append((jnp.logical_and(gives_left, gives_up), jnp.logical_and(has_right, has_below), {"tx": left, "ty": up},
+                   nq, height, N, base, base + nq * short, cuts + 1))
+    pieces += [(gives_left, has_right, {"tx": left}, nq, k * size, size, k * long, k * long, k) for k in range(cuts)]
+    steps = [(gives_up, has_below, {"ty": up}, cuts, cuts, 1),
+             (jnp.logical_and(gives_left, gives_up), jnp.logical_and(has_right, has_below), {"tx": left, "ty": up}, cuts, cuts + 1, 1),
+             (gives_left, has_right, {"tx": left}, 0, 0, cuts)]
+    npieces = len(pieces)
+
+    def strip(n):
+        _, _, where, _, _, rows, out, into, _ = pieces[n]
+        length = rows * 5 // 4
+        return remote(code_out.at[pl.ds(out, length)], code_in.at[pl.ds(into, length)], strip_send.at[n], strip_recv.at[n], where)
+
+    def strip_step(n):
+        _, _, where, out, into, number = steps[n]
+        return remote(step_out.at[pl.ds(out, number)], step_in.at[pl.ds(into, number)],
+                      strip_send.at[npieces + n], strip_recv.at[npieces + n], where)
+
+    def forward(n):
+        place = pl.ds(pieces[n][7], pieces[n][5] * 5 // 4)
+        return remote(code_in.at[place], code_pair.at[place], pair_send.at[n], pair_recv.at[n], peer)
+
+    def forward_step(n):
+        place = pl.ds(steps[n][4], steps[n][5])
+        return remote(step_in.at[place], step_pair.at[place], pair_send.at[npieces + n], pair_recv.at[npieces + n], peer)
+
+    def store(off, number):
+        rows = number.shape[0]
+        code_out[off:off + rows], code_out[off + rows:off + rows * 5 // 4] = split_wide(number)
+
+    for c in mine:
+        c.wait()
+    number, step_out[cuts] = encode_wide(jnp.concatenate([ext_ref[me, q, :N] for q in range(nq)], axis=0))
+    for q in range(nq):
+        store(base + q * short, number[q * N:(q + 1) * N])
+    for k in range(cuts):
+        number, step_out[k] = encode_wide(ext_ref[me, 0, k * size:(k + 1) * size])
+        store(k * long, number)
     for c in places:
         c.wait()
     list_ref[me, 0:1, :slots] = spots[0, 0]
     list_ref[me, 1:2, :slots] = spots[1, 0]
 
-    step = height // cuts
-    has_right, has_below = tx < ntx - 1, ty < nty - 1
-    gives_left, gives_up = tx > 0, ty > 0
-    pieces = [(gives_up, has_below, {"ty": up}, q, height, 0, N, q) for q in range(nq)]
-    pieces.append((jnp.logical_and(gives_left, gives_up), jnp.logical_and(has_right, has_below), {"tx": left, "ty": up}, nq, height, 0, N, 0))
-    pieces += [(gives_left, has_right, {"tx": left}, nq, k * step, k * step, step, 0) for k in range(cuts)]
-
-    def strip(n):
-        _, _, where, q, row, first, size, source = pieces[n]
-        return remote(obj_ref.at[me, pl.ds(first, size), pl.ds(source * N, N)], ext_ref.at[me, q, pl.ds(row, size)],
-                      strip_send.at[n], strip_recv.at[n], where)
-
-    def forward(n):
-        _, _, _, q, row, _, size, _ = pieces[n]
-        place = ext_ref.at[me, q, pl.ds(row, size)]
-        return remote(place, place, pair_send.at[n], pair_recv.at[n], peer)
-
     pl.semaphore_wait(barrier, 7)
-    for n, piece in enumerate(pieces):
-        @pl.when(piece[0])
+    for n in range(3):
+        @pl.when(steps[n][0])
+        def _():
+            strip_step(n).start()
+    for n in range(npieces):
+        @pl.when(pieces[n][0])
         def _():
             strip(n).start()
 
-    extra = len(pieces)
+    extra = npieces + 3
     lists = remote(list_ref.at[me], list_ref.at[me], pair_send.at[extra], pair_recv.at[extra], peer)
     lists.start()
     move = remote(amp_ref.at[pl.ds(moved, slots - moved)], shared_ref.at[pl.ds(0, slots - moved)],
@@ -331,19 +397,40 @@
     def _():
         move.start()
 
-    for n, piece in enumerate(pieces):
-        @pl.when(jnp.logical_not(piece[1]))
-        def _():
-            _, _, _, q, row, _, size, _ = piece
+    for n in range(npieces):
+        @pl.when(jnp.logical_not(pieces[n][1]))
+        def _():
             for p in range(2):
-                ext_ref[p, q, row:row + size] = jnp.zeros((size, N), jnp.float32)
-
-    order = list(range(nq + 1, len(pieces))) + list(range(nq + 1))
+                ext_ref[p, pieces[n][3], pieces[n][4]:pieces[n][4] + pieces[n][5]] = jnp.zeros((pieces[n][5], N), jnp.float32)
+
+    def place(n, p, code, step):
+        _, _, _, q, row, rows, _, off, which = pieces[n]
+        ext_ref[p, q, row:row + rows] = decode_wide(code[off:off + rows], code[off + rows:off + rows * 5 // 4], step[which])
+
+    for n in range(3):
+        @pl.when(steps[n][1])
+        def _():
+            strip_step(n).wait_recv()
+            forward_step(n).start()
+
+    order = list(range(nq + 1, npieces)) + list(range(nq + 1))
     for n in order:
         @pl.when(pieces[n][1])
         def _():
             strip(n).wait_recv()
             forward(n).start()
+            place(n, me, code_in, step_in)
+
+    for n in range(3):
+        @pl.when(steps[n][1])
+        def _():
+            forward_step(n).wait_recv()
+
+    for n in order:
+        @pl.when(pieces[n][1])
+        def _():
+            forward(n).wait_recv()
+            place(n, other, code_pair, step_pair)
 
     for c in local:
         c.wait()
@@ -357,14 +444,23 @@
     def _():
         move.wait_recv()
 
-    for n, piece in enumerate(pieces):
-        @pl.when(piece[0])
+    for n in range(npieces):
+        @pl.when(pieces[n][0])
         def _():
             strip(n).wait_send()
 
-        @pl.when(piece[1])
-        def _():
-            forward(n).wait()
+        @pl.when(pieces[n][1])
+        def _():
+            forward(n).wait_send()
+
+    for n in range(3):
+        @pl.when(steps[n][0])
+        def _():
+            strip_step(n).wait_send()
+
+        @pl.when(steps[n][1])
+        def _():
+            forward_step(n).wait_send()
 
 
 def spread(obj, amp, rows, cols, cuts=4):
@@ -372,10 +468,12 @@
     height, width = obj.shape[1:]
     slots = amp.shape[0]
     nq = width // N
-    pieces = nq + 1 + cuts
+    copies = nq + 1 + cuts + 3
+    total = height * 5 // 4 + (nq + 1) * (N * 5 // 4)
     vmem = pl.BlockSpec(memory_space=pltpu.VMEM)
     hbm = pl.BlockSpec(memory_space=pltpu.HBM)
     dma = pltpu.SemaphoreType.DMA
+    code, step = pltpu.VMEM((total, N), jnp.int16), pltpu.VMEM((cuts + 2, 8, N), jnp.float32)
     return pl.pallas_call(
         functools.partial(spread_kernel, nty, ntx, cuts),
         out_shape=(
@@ -387,11 +485,12 @@
         out_specs=(vmem, vmem, vmem),
         scratch_shapes=[
             pltpu.VMEM((2, 1, 1, slots), jnp.int32),
-            dma((2 * nq + 3,)), dma((pieces,)), dma((pieces,)), dma((pieces + 2,)), dma((pieces + 2,)),
+            code, step, code, step, code, step,
+            dma((2 * nq + 3,)), dma((copies,)), dma((copies,)), dma((copies + 2,)), dma((copies + 2,)),
         ],
-        compiler_params=pltpu.CompilerParams(collective_id=0, has_side_effects=True, vmem_limit_bytes=40 << 20),
+        compiler_params=pltpu.CompilerParams(collective_id=0, has_side_effects=True, vmem_limit_bytes=SPREAD_VMEM),
         name="spread",
-    )(obj, amp, rows, cols)
+    )(*(pltpu.with_memory_space_constraint(x, pltpu.HBM) for x in (obj, amp, rows, cols)))
 
 
 def dft_tables(length):
@@ -496,13 +595,33 @@
     )(counts, lists, ext, probe, amp, fwd, inv)
 
 
+def flush_kernel(a_ref, b_ref, a_out, b_out, sem):
+    copies = [pltpu.make_async_copy(a_ref, a_out, sem.at[0]), pltpu.make_async_copy(b_ref, b_out, sem.at[1])]
+    for c in copies:
+        c.start()
+    for c in copies:
+        c.wait()
+
+
+def flush(a, b):
+    hbm = pl.BlockSpec(memory_space=pltpu.HBM)
+    return pl.pallas_call(
+        flush_kernel,
+        out_shape=(jax.ShapeDtypeStruct(a.shape, a.dtype), jax.ShapeDtypeStruct(b.shape, b.dtype)),
+        in_specs=[pl.BlockSpec(memory_space=pltpu.VMEM)] * 2,
+        out_specs=(hbm, hbm),
+        scratch_shapes=[pltpu.SemaphoreType.DMA((2,))],
+        name="flush",
+    )(*(pltpu.with_memory_space_constraint(x, pltpu.VMEM) for x in (a, b)))
+
+
 def shards(object_field, probe_field, amplitudes, start_row, start_col, counts):
     height, width = object_field.shape[1:]
     extended, shared, lists = spread(object_field, amplitudes[0, 0], start_row, start_col)
     forward, inverse = dft_tables(N)
     grad, probe_part = patches(
         counts, lists, extended, probe_field, shared, jnp.asarray(forward), jnp.asarray(inverse), BLK)
-    return collect(counts, grad, probe_part, height, width)
+    return flush(*collect(counts, grad, probe_part, height, width))
 
 
 def solution(mesh):

time: 77.9 us -> 66.3 us (0.85)
  local copies, waits for them, and re-layouts: 6.48 us -> 0.02 us
  Pallas kernels: 70.6 us -> 65.4 us
    unnamed x18 -> x8, local copies, waits for them, and re-layouts: 6.48 us -> 0.02 us
    pallas_call x1, Pallas kernels: 25.5 us -> 21.6 us  [spread(): pl.pallas_call(functools.partial(spread_kernel, nty, ntx, cuts), out_shap...]
    pallas_call x1, Pallas kernels: 3.99 us -> 0.97 us  [patches(): pl.pallas_call(functools.partial(patch_kernel, B, amp.shape[0] * 2 // 3),...]
    pallas_call x0 -> x1, Pallas kernels: none -> 1.36 us  [flush(): pl.pallas_call(flush_kernel, out_shape=(jax.ShapeDtypeStruct(a.shape, a.d...]
where the time goes in v4:
time: 66.3 us; the launch traced here: 66.2 us
  Pallas kernels  65.4 us (99%)
  between operations  0.72 us (1%)
    pallas_call x1, Pallas kernels, collect(): pl.pallas_call(functools.partial(collect_kernel, nty, ntx, zh, zl), out_s...  41.5 us
    pallas_call x1, Pallas kernels, spread(): pl.pallas_call(functools.partial(spread_kernel, nty, ntx, cuts), out_shap...  21.6 us
    pallas_call x1, Pallas kernels, flush(): pl.pallas_call(flush_kernel, out_shape=(jax.ShapeDtypeStruct(a.shape, a.d...  1.36 us

profile of v4, /device:TPU:1, one launch (start us, length us, event | category | flops | bytes accessed | tf_op | source)
XLA Modules:
  0.0 66.2 jit_solution(15455589816414348828)
XLA Ops:
  0.6 0.0 copy-start
  0.6 0.0 copy-start.1
  0.7 0.0 copy-start.2
  0.7 0.0 copy-start.3
  0.7 21.6 %spread.1 = (f32[2,3,1152,128]{3,2,1,0:T(8,128)S(1)}, bf16[96,128,128]{2,1,0:T(8,128)(2,1)S(1)}, s32[2,8,128]{2,1,0:T(8,128)S(1)}) custom-call(f32[2,1024,256]{2,1,0:T(8,128)} %obj_ref.1, bf16[64,128,128]{2,1,0:T(8,128)(2,1)} %bitcast.1, s32[1,1,64]{2,1,0:T(1,128)} %rows_ref.1, s32[1,1,64]{2,1,0:T(1,128)} %cols_ref.1), custom_call_target="tpu_custom_call" | custom-call | tf_op jit(solution)/shard_map/spread/pallas_call | solution.py:477
  22.3 0.0 copy-done
  22.3 0.0 copy-done.1
  22.3 0.0 copy-done.2
  22.3 0.0 copy-done.3
  22.3 1.0 %patches.1 = (f32[2,3,1152,128]{3,2,1,0:T(8,128)S(1)}, f32[2,128,128]{2,1,0:T(8,128)S(1)}) custom-call(s32[8,16]{1,0:T(8,128)S(1)} %copy-done.3, s32[2,8,128]{2,1,0:T(8,128)S(1)} %get-tuple-element.9.list_ref, f32[2,3,1152,128]{3,2,1,0:T(8,128)S(1)} %get-tuple-element.10.ext_ref, f32[2,128,128]{2,1,0:T(8,128)S(1)} %copy-done, ...), custom_call_target="tpu_custom_call" | custom-call | tf_op jit(solution)/shard_map/patches/pallas_call | solution.py:587
  23.3 41.5 %collect.1 = (f32[2,1024,256]{2,1,0:T(8,128)S(1)}, f32[2,128,128]{2,1,0:T(8,128)S(1)}) custom-call(s32[8,16]{1,0:T(8,128)S(1)} %copy-done.3, f32[2,3,1152,128]{3,2,1,0:T(8,128)S(1)} %get-tuple-element.12.acc_ref, f32[2,128,128]{2,1,0:T(8,128)S(1)} %get-tuple-element.13.pg_ref), custom_call_target="tpu_custom_call" | custom-call | tf_op jit(solution)/shard_map/collect/pallas_call | solution.py:250
  64.8 1.4 %flush.1 = (f32[2,1024,256]{2,1,0:T(8,128)}, f32[2,128,128]{2,1,0:T(8,128)}) custom-call(f32[2,1024,256]{2,1,0:T(8,128)S(1)} %get-tuple-element.14.a_ref, f32[2,128,128]{2,1,0:T(8,128)S(1)} %get-tuple-element.15.b_ref), custom_call_target="tpu_custom_call" | custom-call | tf_op jit(solution)/shard_map/flush/pallas_call | solution.py:608
Async XLA Ops:
  0.6 21.6 %copy-start = (f32[2,128,128]{2,1,0:T(8,128)S(1)}, f32[2,128,128]{2,1,0:T(8,128)}, u32[]{:S(2)}) copy-start(f32[2,128,128]{2,1,0:T(8,128)} %probe_ref.1) | copy-start | bytes 393220
  0.6 21.6 %copy-start.1 = (bf16[256,256]{1,0:T(8,128)(2,1)S(1)}, bf16[256,256]{1,0:T(8,128)(2,1)}, u32[]{:S(2)}) copy-start(bf16[256,256]{1,0:T(8,128)(2,1)} %constant.5.clone.inv_ref) | copy-start | bytes 393220
  0.7 21.6 %copy-start.2 = (bf16[256,256]{1,0:T(8,128)(2,1)S(1)}, bf16[256,256]{1,0:T(8,128)(2,1)}, u32[]{:S(2)}) copy-start(bf16[256,256]{1,0:T(8,128)(2,1)} %constant.4.clone.fwd_ref) | copy-start | bytes 393220
  0.7 21.6 %copy-start.3 = (s32[8,16]{1,0:T(8,128)S(1)}, s32[8,16]{1,0:T(8,128)}, u32[]{:S(2)}) copy-start(s32[8,16]{1,0:T(8,128)} %counts_ref.3) | copy-start | bytes 1540

commit v5 on v4

--- a/solution.py
+++ b/solution.py
@@ -10,7 +10,7 @@
 from jax.experimental.pallas import tpu as pltpu
 from jax.sharding import PartitionSpec as P
 
-BLK = 8
+BLK = 24
 
 N = 128
 LEVELS = 32766.0
@@ -37,29 +37,29 @@
 
 
 def collect_kernel(nty, ntx, zh, zl, counts_ref, acc_ref, pg_ref, out_ref, pgo_ref,
-                   theirs, pg_theirs, code_out, step_out, code_in, step_in, by_line, by_plane, part,
-                   pair_send, pair_recv, strip_send, strip_recv, line_send, line_recv, plane_send, plane_recv, all_send, all_recv):
+                   theirs, pg_theirs, code_out, step_out, code_in, step_in, by_flat, by_deep, part,
+                   pair_send, pair_recv, strip_send, strip_recv, flat_send, flat_recv, deep_send, deep_recv, all_send, all_recv):
     ty, tx, me = lax.axis_index("ty"), lax.axis_index("tx"), lax.axis_index("pa")
     other = 1 - me
     height = out_ref.shape[1]
     nq = out_ref.shape[2] // N
     peer = {"pa": other}
-    nline, nplane = zh * zl, (nty // zh) * (ntx // zl)
-    chunk = N // nline
-    line_id = lax.rem(ty, zh) * zl + lax.rem(tx, zl)
-    plane_id = (ty // zh) * (ntx // zl) + tx // zl
-
-    def in_line(k):
+    nflat, ndeep = (nty // zh) * (ntx // zl), zh * zl
+    chunk = N // nflat
+    deep_id = lax.rem(ty, zh) * zl + lax.rem(tx, zl)
+    flat_id = (ty // zh) * (ntx // zl) + tx // zl
+
+    def in_deep(k):
         return {"ty": (ty // zh) * zh + k // zl, "tx": (tx // zl) * zl + lax.rem(k, zl)}
 
-    def in_plane(k):
+    def in_flat(k):
         return {"ty": (k // (ntx // zl)) * zh + lax.rem(ty, zh), "tx": lax.rem(k, ntx // zl) * zl + lax.rem(tx, zl)}
 
-    def next_in_line(k):
-        return lax.rem(line_id + k, nline)
-
-    def next_in_plane(k):
-        return lax.rem(plane_id + k, nplane)
+    def next_flat(k):
+        return lax.rem(flat_id + k, nflat)
+
+    def next_deep(k):
+        return lax.rem(deep_id + k, ndeep)
 
     sizes = (height, nq * N, N)
     offs = (0, height, height + nq * N)
@@ -74,16 +74,16 @@
     for where in (peer,) + targets + sources:
         pl.semaphore_signal(barrier, inc=1, device_id=where, device_id_type=MESH)
 
-    @pl.loop(1, nline)
-    def _(k):
-        pl.semaphore_signal(barrier, inc=1, device_id=in_line(next_in_line(k)), device_id_type=MESH)
-
-    @pl.loop(1, nplane)
-    def _(k):
-        pl.semaphore_signal(barrier, inc=1, device_id=in_plane(next_in_plane(k)), device_id_type=MESH)
+    @pl.loop(1, nflat)
+    def _(k):
+        pl.semaphore_signal(barrier, inc=1, device_id=in_flat(next_flat(k)), device_id_type=MESH)
+
+    @pl.loop(1, ndeep)
+    def _(k):
+        pl.semaphore_signal(barrier, inc=1, device_id=in_deep(next_deep(k)), device_id_type=MESH)
 
     total = jnp.sum(jnp.sum(counts_ref[...].astype(jnp.float32), axis=1, keepdims=True), axis=0, keepdims=True)
-    pl.semaphore_wait(barrier, 1 + 6 + nline - 1 + nplane - 1)
+    pl.semaphore_wait(barrier, 1 + 6 + nflat - 1 + ndeep - 1)
 
     def swap(n, src, dst):
         return remote(src, dst, pair_send.at[n], pair_recv.at[n], peer)
@@ -116,30 +116,30 @@
     def rows_of(k):
         return pl.ds(pl.multiple_of(k * chunk, chunk), chunk)
 
-    def line_copy(k):
-        return remote(part.at[rows_of(k)], by_line.at[line_id], line_send.at[k], line_recv.at[line_id], in_line(k))
-
-    def line_arrival(k):
-        return remote(part.at[rows_of(k)], by_line.at[k], line_send.at[k], line_recv.at[k], in_line(k))
-
-    def plane_copy(k):
-        return remote(by_plane.at[plane_id], by_plane.at[plane_id], plane_send.at[k], plane_recv.at[plane_id], in_plane(k))
-
-    def plane_arrival(k):
-        return remote(by_plane.at[plane_id], by_plane.at[k], plane_send.at[k], plane_recv.at[k], in_plane(k))
+    def flat_copy(k):
+        return remote(part.at[rows_of(k)], by_flat.at[flat_id], flat_send.at[k], flat_recv.at[flat_id], in_flat(k))
+
+    def flat_arrival(k):
+        return remote(part.at[rows_of(k)], by_flat.at[k], flat_send.at[k], flat_recv.at[k], in_flat(k))
+
+    def deep_copy(k):
+        return remote(by_deep.at[deep_id], by_deep.at[deep_id], deep_send.at[k], deep_recv.at[deep_id], in_deep(k))
+
+    def deep_arrival(k):
+        return remote(by_deep.at[deep_id], by_deep.at[k], deep_send.at[k], deep_recv.at[k], in_deep(k))
 
     def all_copy(k, at):
         place = pgo_ref.at[me, rows_of(at)]
-        return remote(place, place, all_send.at[k], all_recv.at[at], in_line(k))
+        return remote(place, place, all_send.at[k], all_recv.at[at], in_flat(k))
 
     probe_swap.wait()
     part[...] = pg_ref[me] + pg_theirs[...]
 
-    @pl.loop(1, nline)
-    def _(k):
-        line_copy(next_in_line(k)).start()
-
-    by_line[line_id] = part[rows_of(line_id)]
+    @pl.loop(1, nflat)
+    def _(k):
+        flat_copy(next_flat(k)).start()
+
+    by_flat[flat_id] = part[rows_of(flat_id)]
 
     for c in low:
         c.wait()
@@ -148,18 +148,18 @@
     pack(2, acc_ref[me, nq, height:] + theirs[nq, height:])
     pack(0, acc_ref[me, nq, :height] + theirs[nq, :height])
 
-    @pl.loop(1, nline)
-    def _(k):
-        line_arrival(next_in_line(k)).wait_recv()
-
-    mine = by_line[0]
-    for k in range(1, nline):
-        mine = mine + by_line[k]
-    by_plane[plane_id] = mine
-
-    @pl.loop(1, nplane)
-    def _(k):
-        plane_copy(next_in_plane(k)).start()
+    @pl.loop(1, nflat)
+    def _(k):
+        flat_arrival(next_flat(k)).wait_recv()
+
+    mine = by_flat[0]
+    for k in range(1, nflat):
+        mine = mine + by_flat[k]
+    by_deep[deep_id] = mine
+
+    @pl.loop(1, ndeep)
+    def _(k):
+        deep_copy(next_deep(k)).start()
 
     for q in reversed(range(nq)):
         body[q].wait()
@@ -173,18 +173,18 @@
     early = final(2 + 2 * nq, pl.ds(N, height - N), rest)
     early.start()
 
-    @pl.loop(1, nplane)
-    def _(k):
-        plane_arrival(next_in_plane(k)).wait_recv()
-
-    mine = by_plane[0]
-    for k in range(1, nplane):
-        mine = mine + by_plane[k]
-    pgo_ref[me, rows_of(line_id)] = mine / total
-
-    @pl.loop(1, nline)
-    def _(k):
-        all_copy(next_in_line(k), line_id).start()
+    @pl.loop(1, ndeep)
+    def _(k):
+        deep_arrival(next_deep(k)).wait_recv()
+
+    mine = by_deep[0]
+    for k in range(1, ndeep):
+        mine = mine + by_deep[k]
+    pgo_ref[me, rows_of(flat_id)] = mine / total
+
+    @pl.loop(1, nflat)
+    def _(k):
+        all_copy(next_flat(k), flat_id).start()
 
     @pl.when(gets[1])
     def _():
@@ -209,9 +209,9 @@
     for c in late:
         c.start()
 
-    @pl.loop(1, nline)
-    def _(k):
-        at = next_in_line(k)
+    @pl.loop(1, nflat)
+    def _(k):
+        at = next_flat(k)
         all_copy(at, at).wait_recv()
 
     last = swap(5 + 2 * nq, pgo_ref.at[me], pgo_ref.at[me])
@@ -223,15 +223,15 @@
             for c in strip(n):
                 c.wait_send()
 
-    @pl.loop(1, nline)
-    def _(k):
-        at = next_in_line(k)
-        line_copy(at).wait_send()
-        all_copy(at, line_id).wait_send()
-
-    @pl.loop(1, nplane)
-    def _(k):
-        plane_copy(next_in_plane(k)).wait_send()
+    @pl.loop(1, nflat)
+    def _(k):
+        at = next_flat(k)
+        flat_copy(at).wait_send()
+        all_copy(at, flat_id).wait_send()
+
+    @pl.loop(1, ndeep)
+    def _(k):
+        deep_copy(next_deep(k)).wait_send()
 
     early.wait()
     for c in late:
@@ -243,8 +243,8 @@
     nty, ntx = lax.axis_size("ty"), lax.axis_size("tx")
     nq = width // N
     rows = height + nq * N + N
-    nline, nplane = zh * zl, (nty // zh) * (ntx // zl)
-    chunk = N // nline
+    nflat, ndeep = (nty // zh) * (ntx // zl), zh * zl
+    chunk = N // nflat
     vmem = pl.BlockSpec(memory_space=pltpu.VMEM)
     dma = pltpu.SemaphoreType.DMA
     return pl.pallas_call(
@@ -259,11 +259,11 @@
             pltpu.VMEM((3, 8, N), jnp.float32),
             pltpu.VMEM((rows, N), jnp.int16),
             pltpu.VMEM((3, 8, N), jnp.float32),
-            pltpu.VMEM((nline, chunk, N), jnp.float32),
-            pltpu.VMEM((nplane, chunk, N), jnp.float32),
+            pltpu.VMEM((nflat, chunk, N), jnp.float32),
+            pltpu.VMEM((ndeep, chunk, N), jnp.float32),
             pltpu.VMEM((N, N), jnp.float32),
             dma((6 + 2 * nq,)), dma((6 + 2 * nq,)), dma((6,)), dma((6,)),
-            dma((nline,)), dma((nline,)), dma((nplane,)), dma((nplane,)), dma((nline,)), dma((nline,)),
+            dma((nflat,)), dma((nflat,)), dma((ndeep,)), dma((ndeep,)), dma((nflat,)), dma((nflat,)),
         ],
         compiler_params=pltpu.CompilerParams(collective_id=1, has_side_effects=True, vmem_limit_bytes=40 << 20),
         name="collect",
@@ -571,10 +571,13 @@
             tim = tim + (qre * gim - qim * gre)
             obj = (pre * gre + pim * gim, pre * gim - pim * gre)
             high = lane >= s
+            low = lane < s
             for p in range(2):
                 o = pltpu.roll(obj[p], s, 1)
-                acc_ref[p, j, pl.ds(r, N), :] += jnp.where(high, o, 0.0)
-                acc_ref[p, j + 1, pl.ds(r, N), :] += jnp.where(high, 0.0, o)
+                u = acc_ref[p, j, pl.ds(r, N), :]
+                v = acc_ref[p, j + 1, pl.ds(r, N), :]
+                pltpu.store(acc_ref.at[p, j, pl.ds(r, N), :], u + o, mask=high)
+                pltpu.store(acc_ref.at[p, j + 1, pl.ds(r, N), :], v + o, mask=low)
         pg_ref[0] = tre
         pg_ref[1] = tim
         return 0

time: 66.3 us -> 64.2 us (0.968)
  Pallas kernels: 65.4 us -> 63.3 us
    pallas_call x1, Pallas kernels: 41.5 us -> 32.2 us  [collect(): pl.pallas_call(functools.partial(collect_kernel, nty, ntx, zh, zl), out_s...]
    pallas_call x1, Pallas kernels: 0.97 us -> 8.2 us  [patches(): pl.pallas_call(functools.partial(patch_kernel, B, amp.shape[0] * 2 // 3),...]
where the time goes in v5:
time: 64.2 us; the launch traced here: 64.1 us
  Pallas kernels  63.3 us (99%)
  between operations  0.72 us (1%)
    pallas_call x1, Pallas kernels, collect(): pl.pallas_call(functools.partial(collect_kernel, nty, ntx, zh, zl), out_s...  32.2 us
    pallas_call x1, Pallas kernels, spread(): pl.pallas_call(functools.partial(spread_kernel, nty, ntx, cuts), out_shap...  21.6 us
    pallas_call x1, Pallas kernels, patches(): pl.pallas_call(functools.partial(patch_kernel, B, amp.shape[0] * 2 // 3),...  8.2 us
    pallas_call x1, Pallas kernels, flush(): pl.pallas_call(flush_kernel, out_shape=(jax.ShapeDtypeStruct(a.shape, a.d...  1.36 us

profile of v5, /device:TPU:1, one launch (start us, length us, event | category | flops | bytes accessed | tf_op | source)
XLA Modules:
  0.0 64.1 jit_solution(3001342286906059361)
XLA Ops:
  0.6 0.0 copy-start
  0.6 0.0 copy-start.1
  0.7 0.0 copy-start.2
  0.7 0.0 copy-start.3
  0.7 21.6 %spread.1 = (f32[2,3,1152,128]{3,2,1,0:T(8,128)S(1)}, bf16[96,128,128]{2,1,0:T(8,128)(2,1)S(1)}, s32[2,8,128]{2,1,0:T(8,128)S(1)}) custom-call(f32[2,1024,256]{2,1,0:T(8,128)} %obj_ref.1, bf16[64,128,128]{2,1,0:T(8,128)(2,1)} %bitcast.1, s32[1,1,64]{2,1,0:T(1,128)} %rows_ref.1, s32[1,1,64]{2,1,0:T(1,128)} %cols_ref.1), custom_call_target="tpu_custom_call" | custom-call | tf_op jit(solution)/shard_map/spread/pallas_call | solution.py:477
  22.3 0.0 copy-done
  22.3 0.0 copy-done.1
  22.3 0.0 copy-done.2
  22.3 0.0 copy-done.3
  22.3 8.2 %patches.1 = (f32[2,3,1152,128]{3,2,1,0:T(8,128)S(1)}, f32[2,128,128]{2,1,0:T(8,128)S(1)}) custom-call(s32[8,16]{1,0:T(8,128)S(1)} %copy-done.3, s32[2,8,128]{2,1,0:T(8,128)S(1)} %get-tuple-element.9.list_ref, f32[2,3,1152,128]{3,2,1,0:T(8,128)S(1)} %get-tuple-element.10.ext_ref, f32[2,128,128]{2,1,0:T(8,128)S(1)} %copy-done, ...), custom_call_target="tpu_custom_call" | custom-call | tf_op jit(solution)/shard_map/patches/pallas_call | solution.py:590
  30.5 32.2 %collect.1 = (f32[2,1024,256]{2,1,0:T(8,128)S(1)}, f32[2,128,128]{2,1,0:T(8,128)S(1)}) custom-call(s32[8,16]{1,0:T(8,128)S(1)} %copy-done.3, f32[2,3,1152,128]{3,2,1,0:T(8,128)S(1)} %get-tuple-element.12.acc_ref, f32[2,128,128]{2,1,0:T(8,128)S(1)} %get-tuple-element.13.pg_ref), custom_call_target="tpu_custom_call" | custom-call | tf_op jit(solution)/shard_map/collect/pallas_call | solution.py:250
  62.7 1.4 %flush.1 = (f32[2,1024,256]{2,1,0:T(8,128)}, f32[2,128,128]{2,1,0:T(8,128)}) custom-call(f32[2,1024,256]{2,1,0:T(8,128)S(1)} %get-tuple-element.14.a_ref, f32[2,128,128]{2,1,0:T(8,128)S(1)} %get-tuple-element.15.b_ref), custom_call_target="tpu_custom_call" | custom-call | tf_op jit(solution)/shard_map/flush/pallas_call | solution.py:611
Async XLA Ops:
  0.6 21.6 %copy-start = (f32[2,128,128]{2,1,0:T(8,128)S(1)}, f32[2,128,128]{2,1,0:T(8,128)}, u32[]{:S(2)}) copy-start(f32[2,128,128]{2,1,0:T(8,128)} %probe_ref.1) | copy-start | bytes 393220
  0.6 21.6 %copy-start.1 = (bf16[256,256]{1,0:T(8,128)(2,1)S(1)}, bf16[256,256]{1,0:T(8,128)(2,1)}, u32[]{:S(2)}) copy-start(bf16[256,256]{1,0:T(8,128)(2,1)} %constant.5.clone.inv_ref) | copy-start | bytes 393220
  0.7 21.6 %copy-start.2 = (bf16[256,256]{1,0:T(8,128)(2,1)S(1)}, bf16[256,256]{1,0:T(8,128)(2,1)}, u32[]{:S(2)}) copy-start(bf16[256,256]{1,0:T(8,128)(2,1)} %constant.4.clone.fwd_ref) | copy-start | bytes 393220
  0.7 21.6 %copy-start.3 = (s32[8,16]{1,0:T(8,128)S(1)}, s32[8,16]{1,0:T(8,128)}, u32[]{:S(2)}) copy-start(s32[8,16]{1,0:T(8,128)} %counts_ref.3) | copy-start | bytes 1540

commit v6 on v4

--- a/solution.py
+++ b/solution.py
@@ -10,7 +10,7 @@
 from jax.experimental.pallas import tpu as pltpu
 from jax.sharding import PartitionSpec as P
 
-BLK = 8
+BLK = 24
 
 N = 128
 LEVELS = 32766.0
@@ -108,6 +108,7 @@
     def pack(n, value):
         code_out[pl.ds(offs[n], sizes[n])], step_out[n] = encode(value)
 
+    def leave(n):
         @pl.when(sends[n])
         def _():
             for c in strip(n):
@@ -146,6 +147,8 @@
     pack(1, jnp.concatenate([acc_ref[me, q, height:] + theirs[q, height:] for q in range(nq)], axis=0))
     right.wait()
     pack(2, acc_ref[me, nq, height:] + theirs[nq, height:])
+    leave(1)
+    leave(2)
     pack(0, acc_ref[me, nq, :height] + theirs[nq, :height])
 
     @pl.loop(1, nline)
@@ -160,6 +163,8 @@
     @pl.loop(1, nplane)
     def _(k):
         plane_copy(next_in_plane(k)).start()
+
+    leave(0)
 
     for q in reversed(range(nq)):
         body[q].wait()
@@ -571,10 +576,13 @@
             tim = tim + (qre * gim - qim * gre)
             obj = (pre * gre + pim * gim, pre * gim - pim * gre)
             high = lane >= s
+            low = lane < s
             for p in range(2):
                 o = pltpu.roll(obj[p], s, 1)
-                acc_ref[p, j, pl.ds(r, N), :] += jnp.where(high, o, 0.0)
-                acc_ref[p, j + 1, pl.ds(r, N), :] += jnp.where(high, 0.0, o)
+                u = acc_ref[p, j, pl.ds(r, N), :]
+                v = acc_ref[p, j + 1, pl.ds(r, N), :]
+                pltpu.store(acc_ref.at[p, j, pl.ds(r, N), :], u + o, mask=high)
+                pltpu.store(acc_ref.at[p, j + 1, pl.ds(r, N), :], v + o, mask=low)
         pg_ref[0] = tre
         pg_ref[1] = tim
         return 0
@@ -596,7 +604,11 @@
 
 
 def flush_kernel(a_ref, b_ref, a_out, b_out, sem):
-    copies = [pltpu.make_async_copy(a_ref, a_out, sem.at[0]), pltpu.make_async_copy(b_ref, b_out, sem.at[1])]
+    size = a_ref.shape[1] // 4
+    copies = [pltpu.make_async_copy(b_ref, b_out, sem.at[8])]
+    for n in range(8):
+        place = (n // 4, pl.ds(n % 4 * size, size))
+        copies.append(pltpu.make_async_copy(a_ref.at[place], a_out.at[place], sem.at[n]))
     for c in copies:
         c.start()
     for c in copies:
@@ -610,7 +622,7 @@
         out_shape=(jax.ShapeDtypeStruct(a.shape, a.dtype), jax.ShapeDtypeStruct(b.shape, b.dtype)),
         in_specs=[pl.BlockSpec(memory_space=pltpu.VMEM)] * 2,
         out_specs=(hbm, hbm),
-        scratch_shapes=[pltpu.SemaphoreType.DMA((2,))],
+        scratch_shapes=[pltpu.SemaphoreType.DMA((9,))],
         name="flush",
     )(*(pltpu.with_memory_space_constraint(x, pltpu.VMEM) for x in (a, b)))
 

time: 66.3 us -> 63.1 us (0.952)
  Pallas kernels: 65.4 us -> 61.7 us
    pallas_call x1, Pallas kernels: 41.5 us -> 37.8 us  [collect(): pl.pallas_call(functools.partial(collect_kernel, nty, ntx, zh, zl), out_s...]
where the time goes in v6:
time: 63.1 us; the launch traced here: 62.5 us
  Pallas kernels  61.7 us (98%)
  between operations  0.72 us (1%)
    pallas_call x1, Pallas kernels, collect(): pl.pallas_call(functools.partial(collect_kernel, nty, ntx, zh, zl), out_s...  37.8 us
    pallas_call x1, Pallas kernels, spread(): pl.pallas_call(functools.partial(spread_kernel, nty, ntx, cuts), out_shap...  21.6 us
    pallas_call x1, Pallas kernels, flush(): pl.pallas_call(flush_kernel, out_shape=(jax.ShapeDtypeStruct(a.shape, a.d...  1.43 us

profile of v6, /device:TPU:1, one launch (start us, length us, event | category | flops | bytes accessed | tf_op | source)
XLA Modules:
  0.0 62.5 jit_solution(1176648411635814680)
XLA Ops:
  0.6 0.0 copy-start
  0.6 0.0 copy-start.1
  0.7 0.0 copy-start.2
  0.7 0.0 copy-start.3
  0.7 21.6 %spread.1 = (f32[2,3,1152,128]{3,2,1,0:T(8,128)S(1)}, bf16[96,128,128]{2,1,0:T(8,128)(2,1)S(1)}, s32[2,8,128]{2,1,0:T(8,128)S(1)}) custom-call(f32[2,1024,256]{2,1,0:T(8,128)} %obj_ref.1, bf16[64,128,128]{2,1,0:T(8,128)(2,1)} %bitcast.1, s32[1,1,64]{2,1,0:T(1,128)} %rows_ref.1, s32[1,1,64]{2,1,0:T(1,128)} %cols_ref.1), custom_call_target="tpu_custom_call" | custom-call | tf_op jit(solution)/shard_map/spread/pallas_call | solution.py:482
  22.3 0.0 copy-done
  22.3 0.0 copy-done.1
  22.3 0.0 copy-done.2
  22.3 0.0 copy-done.3
  22.3 1.0 %patches.1 = (f32[2,3,1152,128]{3,2,1,0:T(8,128)S(1)}, f32[2,128,128]{2,1,0:T(8,128)S(1)}) custom-call(s32[8,16]{1,0:T(8,128)S(1)} %copy-done.3, s32[2,8,128]{2,1,0:T(8,128)S(1)} %get-tuple-element.9.list_ref, f32[2,3,1152,128]{3,2,1,0:T(8,128)S(1)} %get-tuple-element.10.ext_ref, f32[2,128,128]{2,1,0:T(8,128)S(1)} %copy-done, ...), custom_call_target="tpu_custom_call" | custom-call | tf_op jit(solution)/shard_map/patches/pallas_call | solution.py:595
  23.3 37.8 %collect.1 = (f32[2,1024,256]{2,1,0:T(8,128)S(1)}, f32[2,128,128]{2,1,0:T(8,128)S(1)}) custom-call(s32[8,16]{1,0:T(8,128)S(1)} %copy-done.3, f32[2,3,1152,128]{3,2,1,0:T(8,128)S(1)} %get-tuple-element.12.acc_ref, f32[2,128,128]{2,1,0:T(8,128)S(1)} %get-tuple-element.13.pg_ref), custom_call_target="tpu_custom_call" | custom-call | tf_op jit(solution)/shard_map/collect/pallas_call | solution.py:255
  61.1 1.4 %flush.1 = (f32[2,1024,256]{2,1,0:T(8,128)}, f32[2,128,128]{2,1,0:T(8,128)}) custom-call(f32[2,1024,256]{2,1,0:T(8,128)S(1)} %get-tuple-element.14.a_ref, f32[2,128,128]{2,1,0:T(8,128)S(1)} %get-tuple-element.15.b_ref), custom_call_target="tpu_custom_call" | custom-call | tf_op jit(solution)/shard_map/flush/pallas_call | solution.py:620
Async XLA Ops:
  0.6 21.6 %copy-start = (f32[2,128,128]{2,1,0:T(8,128)S(1)}, f32[2,128,128]{2,1,0:T(8,128)}, u32[]{:S(2)}) copy-start(f32[2,128,128]{2,1,0:T(8,128)} %probe_ref.1) | copy-start | bytes 393220
  0.6 21.6 %copy-start.1 = (bf16[256,256]{1,0:T(8,128)(2,1)S(1)}, bf16[256,256]{1,0:T(8,128)(2,1)}, u32[]{:S(2)}) copy-start(bf16[256,256]{1,0:T(8,128)(2,1)} %constant.5.clone.inv_ref) | copy-start | bytes 393220
  0.7 21.6 %copy-start.2 = (bf16[256,256]{1,0:T(8,128)(2,1)S(1)}, bf16[256,256]{1,0:T(8,128)(2,1)}, u32[]{:S(2)}) copy-start(bf16[256,256]{1,0:T(8,128)(2,1)} %constant.4.clone.fwd_ref) | copy-start | bytes 393220
  0.7 21.6 %copy-start.3 = (s32[8,16]{1,0:T(8,128)S(1)}, s32[8,16]{1,0:T(8,128)}, u32[]{:S(2)}) copy-start(s32[8,16]{1,0:T(8,128)} %counts_ref.3) | copy-start | bytes 1540

commit v7 on v6

--- a/solution.py
+++ b/solution.py
@@ -37,7 +37,7 @@
 
 
 def collect_kernel(nty, ntx, zh, zl, counts_ref, acc_ref, pg_ref, out_ref, pgo_ref,
-                   theirs, pg_theirs, code_out, step_out, code_in, step_in, by_line, by_plane, part,
+                   theirs, code_out, step_out, code_in, step_in, by_line, by_plane,
                    pair_send, pair_recv, strip_send, strip_recv, line_send, line_recv, plane_send, plane_recv, all_send, all_recv):
     ty, tx, me = lax.axis_index("ty"), lax.axis_index("tx"), lax.axis_index("pa")
     other = 1 - me
@@ -49,14 +49,18 @@
     line_id = lax.rem(ty, zh) * zl + lax.rem(tx, zl)
     plane_id = (ty // zh) * (ntx // zl) + tx // zl
 
-    def in_line(k):
-        return {"ty": (ty // zh) * zh + k // zl, "tx": (tx // zl) * zl + lax.rem(k, zl)}
+    nmember = 2 * nline
+    member_id = me * nline + line_id
+
+    def in_line(a):
+        k = lax.rem(a, nline)
+        return {"ty": (ty // zh) * zh + k // zl, "tx": (tx // zl) * zl + lax.rem(k, zl), "pa": a // nline}
 
     def in_plane(k):
         return {"ty": (k // (ntx // zl)) * zh + lax.rem(ty, zh), "tx": lax.rem(k, ntx // zl) * zl + lax.rem(tx, zl)}
 
     def next_in_line(k):
-        return lax.rem(line_id + k, nline)
+        return lax.rem(member_id + k, nmember)
 
     def next_in_plane(k):
         return lax.rem(plane_id + k, nplane)
@@ -71,10 +75,10 @@
     gets = (tx > 0, ty > 0, jnp.logical_and(tx > 0, ty > 0))
 
     barrier = pltpu.get_barrier_semaphore()
-    for where in (peer,) + targets + sources:
+    for where in targets + sources:
         pl.semaphore_signal(barrier, inc=1, device_id=where, device_id_type=MESH)
 
-    @pl.loop(1, nline)
+    @pl.loop(1, nmember)
     def _(k):
         pl.semaphore_signal(barrier, inc=1, device_id=in_line(next_in_line(k)), device_id_type=MESH)
 
@@ -83,16 +87,30 @@
         pl.semaphore_signal(barrier, inc=1, device_id=in_plane(next_in_plane(k)), device_id_type=MESH)
 
     total = jnp.sum(jnp.sum(counts_ref[...].astype(jnp.float32), axis=1, keepdims=True), axis=0, keepdims=True)
-    pl.semaphore_wait(barrier, 1 + 6 + nline - 1 + nplane - 1)
+    pl.semaphore_wait(barrier, 6 + nmember - 1 + nplane - 1)
+
+    def rows_of(k):
+        return pl.ds(pl.multiple_of(k * chunk, chunk), chunk)
+
+    def line_copy(a):
+        return remote(pg_ref.at[a // nline, rows_of(lax.rem(a, nline))], by_line.at[member_id],
+                      line_send.at[a], line_recv.at[member_id], in_line(a))
+
+    def line_arrival(a):
+        return remote(pg_ref.at[me, rows_of(line_id)], by_line.at[a], line_send.at[a], line_recv.at[a], in_line(a))
+
+    @pl.loop(1, nmember)
+    def _(k):
+        line_copy(next_in_line(k)).start()
+
+    by_line[member_id] = pg_ref[me, rows_of(line_id)]
 
     def swap(n, src, dst):
         return remote(src, dst, pair_send.at[n], pair_recv.at[n], peer)
 
-    probe_swap = swap(1 + nq, pg_ref.at[other], pg_theirs)
     right = swap(0, acc_ref.at[other, nq], theirs.at[nq])
     low = [swap(1 + q, acc_ref.at[other, q, pl.ds(height, N)], theirs.at[q, pl.ds(height, N)]) for q in range(nq)]
     body = [swap(2 + nq + q, acc_ref.at[other, q, pl.ds(0, height)], theirs.at[q, pl.ds(0, height)]) for q in range(nq)]
-    probe_swap.start()
     for c in low:
         c.start()
     right.start()
@@ -114,33 +132,15 @@
             for c in strip(n):
                 c.start()
 
-    def rows_of(k):
-        return pl.ds(pl.multiple_of(k * chunk, chunk), chunk)
-
-    def line_copy(k):
-        return remote(part.at[rows_of(k)], by_line.at[line_id], line_send.at[k], line_recv.at[line_id], in_line(k))
-
-    def line_arrival(k):
-        return remote(part.at[rows_of(k)], by_line.at[k], line_send.at[k], line_recv.at[k], in_line(k))
-
     def plane_copy(k):
         return remote(by_plane.at[plane_id], by_plane.at[plane_id], plane_send.at[k], plane_recv.at[plane_id], in_plane(k))
 
     def plane_arrival(k):
         return remote(by_plane.at[plane_id], by_plane.at[k], plane_send.at[k], plane_recv.at[k], in_plane(k))
 
-    def all_copy(k, at):
-        place = pgo_ref.at[me, rows_of(at)]
-        return remote(place, place, all_send.at[k], all_recv.at[at], in_line(k))
-
-    probe_swap.wait()
-    part[...] = pg_ref[me] + pg_theirs[...]
-
-    @pl.loop(1, nline)
-    def _(k):
-        line_copy(next_in_line(k)).start()
-
-    by_line[line_id] = part[rows_of(line_id)]
+    def all_copy(a, source):
+        place = pgo_ref.at[source // nline, rows_of(lax.rem(source, nline))]
+        return remote(place, place, all_send.at[a], all_recv.at[source], in_line(a))
 
     for c in low:
         c.wait()
@@ -151,12 +151,12 @@
     leave(2)
     pack(0, acc_ref[me, nq, :height] + theirs[nq, :height])
 
-    @pl.loop(1, nline)
+    @pl.loop(1, nmember)
     def _(k):
         line_arrival(next_in_line(k)).wait_recv()
 
     mine = by_line[0]
-    for k in range(1, nline):
+    for k in range(1, nmember):
         mine = mine + by_line[k]
     by_plane[plane_id] = mine
 
@@ -187,9 +187,9 @@
         mine = mine + by_plane[k]
     pgo_ref[me, rows_of(line_id)] = mine / total
 
-    @pl.loop(1, nline)
-    def _(k):
-        all_copy(next_in_line(k), line_id).start()
+    @pl.loop(1, nmember)
+    def _(k):
+        all_copy(next_in_line(k), member_id).start()
 
     @pl.when(gets[1])
     def _():
@@ -214,25 +214,22 @@
     for c in late:
         c.start()
 
-    @pl.loop(1, nline)
+    @pl.loop(1, nmember)
     def _(k):
         at = next_in_line(k)
         all_copy(at, at).wait_recv()
 
-    last = swap(5 + 2 * nq, pgo_ref.at[me], pgo_ref.at[me])
-    last.start()
-
     for n in range(3):
         @pl.when(sends[n])
         def _():
             for c in strip(n):
                 c.wait_send()
 
-    @pl.loop(1, nline)
+    @pl.loop(1, nmember)
     def _(k):
         at = next_in_line(k)
         line_copy(at).wait_send()
-        all_copy(at, line_id).wait_send()
+        all_copy(at, member_id).wait_send()
 
     @pl.loop(1, nplane)
     def _(k):
@@ -241,7 +238,6 @@
     early.wait()
     for c in late:
         c.wait()
-    last.wait()
 
 
 def collect(counts, acc, pg, height, width, zh=2, zl=4):
@@ -259,16 +255,14 @@
         out_specs=(vmem, vmem),
         scratch_shapes=[
             pltpu.VMEM((nq + 1, height + N, N), jnp.float32),
-            pltpu.VMEM((N, N), jnp.float32),
             pltpu.VMEM((rows, N), jnp.int16),
             pltpu.VMEM((3, 8, N), jnp.float32),
             pltpu.VMEM((rows, N), jnp.int16),
             pltpu.VMEM((3, 8, N), jnp.float32),
-            pltpu.VMEM((nline, chunk, N), jnp.float32),
+            pltpu.VMEM((2 * nline, chunk, N), jnp.float32),
             pltpu.VMEM((nplane, chunk, N), jnp.float32),
-            pltpu.VMEM((N, N), jnp.float32),
             dma((6 + 2 * nq,)), dma((6 + 2 * nq,)), dma((6,)), dma((6,)),
-            dma((nline,)), dma((nline,)), dma((nplane,)), dma((nplane,)), dma((nline,)), dma((nline,)),
+            dma((2 * nline,)), dma((2 * nline,)), dma((nplane,)), dma((nplane,)), dma((2 * nline,)), dma((2 * nline,)),
         ],
         compiler_params=pltpu.CompilerParams(collective_id=1, has_side_effects=True, vmem_limit_bytes=40 << 20),
         name="collect",

time: 63.1 us -> 63.7 us (level)
  Pallas kernels: 61.7 us -> 62.9 us
    pallas_call x1, Pallas kernels: 37.8 us -> 38.9 us  [collect(): pl.pallas_call(functools.partial(collect_kernel, nty, ntx, zh, zl), out_s...]
where the time goes in v7:
time: 63.7 us
  Pallas kernels  62.9 us (99%)
  between operations  0.72 us (1%)
    pallas_call x1, Pallas kernels, collect(): pl.pallas_call(functools.partial(collect_kernel, nty, ntx, zh, zl), out_s...  38.9 us
    pallas_call x1, Pallas kernels, spread(): pl.pallas_call(functools.partial(spread_kernel, nty, ntx, cuts), out_shap...  21.6 us
    pallas_call x1, Pallas kernels, flush(): pl.pallas_call(flush_kernel, out_shape=(jax.ShapeDtypeStruct(a.shape, a.d...  1.43 us

profile of v7, /device:TPU:1, one launch (start us, length us, event | category | flops | bytes accessed | tf_op | source)
XLA Modules:
  0.0 63.7 jit_solution(4683434918100158902)
XLA Ops:
  0.6 0.0 copy-start
  0.6 0.0 copy-start.1
  0.7 0.0 copy-start.2
  0.7 0.0 copy-start.3
  0.7 21.6 %spread.1 = (f32[2,3,1152,128]{3,2,1,0:T(8,128)S(1)}, bf16[96,128,128]{2,1,0:T(8,128)(2,1)S(1)}, s32[2,8,128]{2,1,0:T(8,128)S(1)}) custom-call(f32[2,1024,256]{2,1,0:T(8,128)} %obj_ref.1, bf16[64,128,128]{2,1,0:T(8,128)(2,1)} %bitcast.1, s32[1,1,64]{2,1,0:T(1,128)} %rows_ref.1, s32[1,1,64]{2,1,0:T(1,128)} %cols_ref.1), custom_call_target="tpu_custom_call" | custom-call | tf_op jit(solution)/shard_map/spread/pallas_call | solution.py:476
  22.3 0.0 copy-done
  22.3 0.0 copy-done.1
  22.3 0.0 copy-done.2
  22.3 0.0 copy-done.3
  22.3 1.0 %patches.1 = (f32[2,3,1152,128]{3,2,1,0:T(8,128)S(1)}, f32[2,128,128]{2,1,0:T(8,128)S(1)}) custom-call(s32[8,16]{1,0:T(8,128)S(1)} %copy-done.3, s32[2,8,128]{2,1,0:T(8,128)S(1)} %get-tuple-element.9.list_ref, f32[2,3,1152,128]{3,2,1,0:T(8,128)S(1)} %get-tuple-element.10.ext_ref, f32[2,128,128]{2,1,0:T(8,128)S(1)} %copy-done, ...), custom_call_target="tpu_custom_call" | custom-call | tf_op jit(solution)/shard_map/patches/pallas_call | solution.py:589
  23.3 38.9 %collect.1 = (f32[2,1024,256]{2,1,0:T(8,128)S(1)}, f32[2,128,128]{2,1,0:T(8,128)S(1)}) custom-call(s32[8,16]{1,0:T(8,128)S(1)} %copy-done.3, f32[2,3,1152,128]{3,2,1,0:T(8,128)S(1)} %get-tuple-element.12.acc_ref, f32[2,128,128]{2,1,0:T(8,128)S(1)} %get-tuple-element.13.pg_ref), custom_call_target="tpu_custom_call" | custom-call | tf_op jit(solution)/shard_map/collect/pallas_call | solution.py:251
  62.2 1.4 %flush.1 = (f32[2,1024,256]{2,1,0:T(8,128)}, f32[2,128,128]{2,1,0:T(8,128)}) custom-call(f32[2,1024,256]{2,1,0:T(8,128)S(1)} %get-tuple-element.14.a_ref, f32[2,128,128]{2,1,0:T(8,128)S(1)} %get-tuple-element.15.b_ref), custom_call_target="tpu_custom_call" | custom-call | tf_op jit(solution)/shard_map/flush/pallas_call | solution.py:614
Async XLA Ops:
  0.6 21.6 %copy-start = (f32[2,128,128]{2,1,0:T(8,128)S(1)}, f32[2,128,128]{2,1,0:T(8,128)}, u32[]{:S(2)}) copy-start(f32[2,128,128]{2,1,0:T(8,128)} %probe_ref.1) | copy-start | bytes 393220
  0.6 21.6 %copy-start.1 = (bf16[256,256]{1,0:T(8,128)(2,1)S(1)}, bf16[256,256]{1,0:T(8,128)(2,1)}, u32[]{:S(2)}) copy-start(bf16[256,256]{1,0:T(8,128)(2,1)} %constant.5.clone.inv_ref) | copy-start | bytes 393220
  0.7 21.6 %copy-start.2 = (bf16[256,256]{1,0:T(8,128)(2,1)S(1)}, bf16[256,256]{1,0:T(8,128)(2,1)}, u32[]{:S(2)}) copy-start(bf16[256,256]{1,0:T(8,128)(2,1)} %constant.4.clone.fwd_ref) | copy-start | bytes 393220
  0.7 21.6 %copy-start.3 = (s32[8,16]{1,0:T(8,128)S(1)}, s32[8,16]{1,0:T(8,128)}, u32[]{:S(2)}) copy-start(s32[8,16]{1,0:T(8,128)} %counts_ref.3) | copy-start | bytes 1540

commit v8 on v6

--- a/solution.py
+++ b/solution.py
@@ -468,7 +468,7 @@
             forward_step(n).wait_send()
 
 
-def spread(obj, amp, rows, cols, cuts=4):
+def spread(obj, amp, rows, cols, cuts=2):
     nty, ntx = lax.axis_size("ty"), lax.axis_size("tx")
     height, width = obj.shape[1:]
     slots = amp.shape[0]

time: 63.1 us -> 62.2 us (0.986)
    pallas_call x1, Pallas kernels: 37.8 us -> 30.2 us  [collect(): pl.pallas_call(functools.partial(collect_kernel, nty, ntx, zh, zl), out_s...]
    pallas_call x1, Pallas kernels: 0.97 us -> 8.29 us  [patches(): pl.pallas_call(functools.partial(patch_kernel, B, amp.shape[0] * 2 // 3),...]
where the time goes in v8:
time: 62.2 us; the launch traced here: 62.1 us
  Pallas kernels  61.4 us (99%)
  between operations  0.72 us (1%)
    pallas_call x1, Pallas kernels, collect(): pl.pallas_call(functools.partial(collect_kernel, nty, ntx, zh, zl), out_s...  30.2 us
    pallas_call x1, Pallas kernels, spread(): pl.pallas_call(functools.partial(spread_kernel, nty, ntx, cuts), out_shap...  21.4 us
    pallas_call x1, Pallas kernels, patches(): pl.pallas_call(functools.partial(patch_kernel, B, amp.shape[0] * 2 // 3),...  8.29 us
    pallas_call x1, Pallas kernels, flush(): pl.pallas_call(flush_kernel, out_shape=(jax.ShapeDtypeStruct(a.shape, a.d...  1.43 us

profile of v8, /device:TPU:1, one launch (start us, length us, event | category | flops | bytes accessed | tf_op | source)
XLA Modules:
  0.0 62.1 jit_solution(2687360595117505504)
XLA Ops:
  0.6 0.0 copy-start
  0.6 0.0 copy-start.1
  0.7 0.0 copy-start.2
  0.7 0.0 copy-start.3
  0.7 21.4 %spread.1 = (f32[2,3,1152,128]{3,2,1,0:T(8,128)S(1)}, bf16[96,128,128]{2,1,0:T(8,128)(2,1)S(1)}, s32[2,8,128]{2,1,0:T(8,128)S(1)}) custom-call(f32[2,1024,256]{2,1,0:T(8,128)} %obj_ref.1, bf16[64,128,128]{2,1,0:T(8,128)(2,1)} %bitcast.1, s32[1,1,64]{2,1,0:T(1,128)} %rows_ref.1, s32[1,1,64]{2,1,0:T(1,128)} %cols_ref.1), custom_call_target="tpu_custom_call" | custom-call | tf_op jit(solution)/shard_map/spread/pallas_call | solution.py:482
  22.1 0.0 copy-done
  22.1 0.0 copy-done.1
  22.1 0.0 copy-done.2
  22.2 0.0 copy-done.3
  22.2 8.3 %patches.1 = (f32[2,3,1152,128]{3,2,1,0:T(8,128)S(1)}, f32[2,128,128]{2,1,0:T(8,128)S(1)}) custom-call(s32[8,16]{1,0:T(8,128)S(1)} %copy-done.3, s32[2,8,128]{2,1,0:T(8,128)S(1)} %get-tuple-element.9.list_ref, f32[2,3,1152,128]{3,2,1,0:T(8,128)S(1)} %get-tuple-element.10.ext_ref, f32[2,128,128]{2,1,0:T(8,128)S(1)} %copy-done, ...), custom_call_target="tpu_custom_call" | custom-call | tf_op jit(solution)/shard_map/patches/pallas_call | solution.py:595
  30.5 30.2 %collect.1 = (f32[2,1024,256]{2,1,0:T(8,128)S(1)}, f32[2,128,128]{2,1,0:T(8,128)S(1)}) custom-call(s32[8,16]{1,0:T(8,128)S(1)} %copy-done.3, f32[2,3,1152,128]{3,2,1,0:T(8,128)S(1)} %get-tuple-element.12.acc_ref, f32[2,128,128]{2,1,0:T(8,128)S(1)} %get-tuple-element.13.pg_ref), custom_call_target="tpu_custom_call" | custom-call | tf_op jit(solution)/shard_map/collect/pallas_call | solution.py:255
  60.7 1.4 %flush.1 = (f32[2,1024,256]{2,1,0:T(8,128)}, f32[2,128,128]{2,1,0:T(8,128)}) custom-call(f32[2,1024,256]{2,1,0:T(8,128)S(1)} %get-tuple-element.14.a_ref, f32[2,128,128]{2,1,0:T(8,128)S(1)} %get-tuple-element.15.b_ref), custom_call_target="tpu_custom_call" | custom-call | tf_op jit(solution)/shard_map/flush/pallas_call | solution.py:620
Async XLA Ops:
  0.6 21.5 %copy-start = (f32[2,128,128]{2,1,0:T(8,128)S(1)}, f32[2,128,128]{2,1,0:T(8,128)}, u32[]{:S(2)}) copy-start(f32[2,128,128]{2,1,0:T(8,128)} %probe_ref.1) | copy-start | bytes 393220
  0.6 21.5 %copy-start.1 = (bf16[256,256]{1,0:T(8,128)(2,1)S(1)}, bf16[256,256]{1,0:T(8,128)(2,1)}, u32[]{:S(2)}) copy-start(bf16[256,256]{1,0:T(8,128)(2,1)} %constant.5.clone.inv_ref) | copy-start | bytes 393220
  0.7 21.5 %copy-start.2 = (bf16[256,256]{1,0:T(8,128)(2,1)S(1)}, bf16[256,256]{1,0:T(8,128)(2,1)}, u32[]{:S(2)}) copy-start(bf16[256,256]{1,0:T(8,128)(2,1)} %constant.4.clone.fwd_ref) | copy-start | bytes 393220
  0.7 21.5 %copy-start.3 = (s32[8,16]{1,0:T(8,128)S(1)}, s32[8,16]{1,0:T(8,128)}, u32[]{:S(2)}) copy-start(s32[8,16]{1,0:T(8,128)} %counts_ref.3) | copy-start | bytes 1540

commit v9 on v6

--- a/solution.py
+++ b/solution.py
@@ -198,6 +198,9 @@
         for q in range(nq):
             out_ref[me, :N, q * N:(q + 1) * N] += decode(code_in[pl.ds(offs[1] + q * N, N)], step_in[1])
 
+    top = final(4 + 2 * nq, pl.ds(0, N), rest)
+    top.start()
+
     @pl.when(gets[2])
     def _():
         for c in strip(2):
@@ -210,9 +213,8 @@
             c.wait_recv()
         out_ref[me, :, :N] += decode(code_in[pl.ds(0, height)], step_in[0])
 
-    late = [final(3 + 2 * nq, pl.ds(0, height), pl.ds(0, N)), final(4 + 2 * nq, pl.ds(0, N), rest)]
-    for c in late:
-        c.start()
+    late = [final(3 + 2 * nq, pl.ds(0, height), pl.ds(0, N)), top]
+    late[0].start()
 
     @pl.loop(1, nline)
     def _(k):

time: 63.1 us -> 62.8 us (level)
    pallas_call x1, Pallas kernels: 37.8 us -> 30.1 us  [collect(): pl.pallas_call(functools.partial(collect_kernel, nty, ntx, zh, zl), out_s...]
    pallas_call x1, Pallas kernels: 0.97 us -> 8.33 us  [patches(): pl.pallas_call(functools.partial(patch_kernel, B, amp.shape[0] * 2 // 3),...]
where the time goes in v9:
time: 62.8 us; the launch traced here: 62.2 us
  Pallas kernels  61.4 us (98%)
  between operations  0.72 us (1%)
    pallas_call x1, Pallas kernels, collect(): pl.pallas_call(functools.partial(collect_kernel, nty, ntx, zh, zl), out_s...  30.1 us
    pallas_call x1, Pallas kernels, spread(): pl.pallas_call(functools.partial(spread_kernel, nty, ntx, cuts), out_shap...  21.6 us
    pallas_call x1, Pallas kernels, patches(): pl.pallas_call(functools.partial(patch_kernel, B, amp.shape[0] * 2 // 3),...  8.33 us
    pallas_call x1, Pallas kernels, flush(): pl.pallas_call(flush_kernel, out_shape=(jax.ShapeDtypeStruct(a.shape, a.d...  1.43 us

profile of v9, /device:TPU:1, one launch (start us, length us, event | category | flops | bytes accessed | tf_op | source)
XLA Modules:
  0.0 62.2 jit_solution(2521980899314610890)
XLA Ops:
  0.6 0.0 copy-start
  0.6 0.0 copy-start.1
  0.7 0.0 copy-start.2
  0.7 0.0 copy-start.3
  0.7 21.6 %spread.1 = (f32[2,3,1152,128]{3,2,1,0:T(8,128)S(1)}, bf16[96,128,128]{2,1,0:T(8,128)(2,1)S(1)}, s32[2,8,128]{2,1,0:T(8,128)S(1)}) custom-call(f32[2,1024,256]{2,1,0:T(8,128)} %obj_ref.1, bf16[64,128,128]{2,1,0:T(8,128)(2,1)} %bitcast.1, s32[1,1,64]{2,1,0:T(1,128)} %rows_ref.1, s32[1,1,64]{2,1,0:T(1,128)} %cols_ref.1), custom_call_target="tpu_custom_call" | custom-call | tf_op jit(solution)/shard_map/spread/pallas_call | solution.py:484
  22.3 0.0 copy-done
  22.3 0.0 copy-done.1
  22.3 0.0 copy-done.2
  22.3 0.0 copy-done.3
  22.3 8.3 %patches.1 = (f32[2,3,1152,128]{3,2,1,0:T(8,128)S(1)}, f32[2,128,128]{2,1,0:T(8,128)S(1)}) custom-call(s32[8,16]{1,0:T(8,128)S(1)} %copy-done.3, s32[2,8,128]{2,1,0:T(8,128)S(1)} %get-tuple-element.9.list_ref, f32[2,3,1152,128]{3,2,1,0:T(8,128)S(1)} %get-tuple-element.10.ext_ref, f32[2,128,128]{2,1,0:T(8,128)S(1)} %copy-done, ...), custom_call_target="tpu_custom_call" | custom-call | tf_op jit(solution)/shard_map/patches/pallas_call | solution.py:597
  30.6 30.1 %collect.1 = (f32[2,1024,256]{2,1,0:T(8,128)S(1)}, f32[2,128,128]{2,1,0:T(8,128)S(1)}) custom-call(s32[8,16]{1,0:T(8,128)S(1)} %copy-done.3, f32[2,3,1152,128]{3,2,1,0:T(8,128)S(1)} %get-tuple-element.12.acc_ref, f32[2,128,128]{2,1,0:T(8,128)S(1)} %get-tuple-element.13.pg_ref), custom_call_target="tpu_custom_call" | custom-call | tf_op jit(solution)/shard_map/collect/pallas_call | solution.py:257
  60.7 1.4 %flush.1 = (f32[2,1024,256]{2,1,0:T(8,128)}, f32[2,128,128]{2,1,0:T(8,128)}) custom-call(f32[2,1024,256]{2,1,0:T(8,128)S(1)} %get-tuple-element.14.a_ref, f32[2,128,128]{2,1,0:T(8,128)S(1)} %get-tuple-element.15.b_ref), custom_call_target="tpu_custom_call" | custom-call | tf_op jit(solution)/shard_map/flush/pallas_call | solution.py:622
Async XLA Ops:
  0.6 21.6 %copy-start = (f32[2,128,128]{2,1,0:T(8,128)S(1)}, f32[2,128,128]{2,1,0:T(8,128)}, u32[]{:S(2)}) copy-start(f32[2,128,128]{2,1,0:T(8,128)} %probe_ref.1) | copy-start | bytes 393220
  0.6 21.6 %copy-start.1 = (bf16[256,256]{1,0:T(8,128)(2,1)S(1)}, bf16[256,256]{1,0:T(8,128)(2,1)}, u32[]{:S(2)}) copy-start(bf16[256,256]{1,0:T(8,128)(2,1)} %constant.5.clone.inv_ref) | copy-start | bytes 393220
  0.7 21.6 %copy-start.2 = (bf16[256,256]{1,0:T(8,128)(2,1)S(1)}, bf16[256,256]{1,0:T(8,128)(2,1)}, u32[]{:S(2)}) copy-start(bf16[256,256]{1,0:T(8,128)(2,1)} %constant.4.clone.fwd_ref) | copy-start | bytes 393220
  0.7 21.6 %copy-start.3 = (s32[8,16]{1,0:T(8,128)S(1)}, s32[8,16]{1,0:T(8,128)}, u32[]{:S(2)}) copy-start(s32[8,16]{1,0:T(8,128)} %counts_ref.3) | copy-start | bytes 1540
